TPU v7x, 32 devices: a whole 2x2x4 slice. The times are simulated.
32 devices in a mesh: blk: 4 (over y, core), group: 8 (over z, x).
Axes of the slice: x: 2, y: 2, z: 4, core: 2. Of those that a mesh axis runs over, the one named last changes fastest.
Arguments:
- queries: bfloat16 [32, 16, 128], P(('blk', 'group')), may hold values from -2.5 to 2.5
- query_mask: int32 [32, 16], P(('blk', 'group')), may hold values from 0 to 1, as said below
- positive: int32 [32], P(('blk', 'group')), may hold values from 0 to 63
- page_vectors: bfloat16 [64, 128, 128], P(('blk', 'group')), may hold values from -2 to 2
- page_mask: int32 [64, 128], P(('blk', 'group')), may hold values from 0 to 1, as said below
Outputs:
- grad_queries: float32 [32, 16, 128], P(('blk', 'group'))
- grad_pages: float32 [64, 128, 128], P(('blk', 'group'))
- mean_loss: float32 [], replicated
Inputs may be any that keep to these rules, and one draw needn't show every extreme that they name: `query_mask`: each row holds ones on its first 8 to 16 token slots and zeros after them. `page_mask`: each row holds ones on its first 32 to 128 patch slots and zeros after them.
All inputs are finite; a program needn't handle non-finite values.
Results may differ from a plain program's by a relative error of at most 0.0028.
Values may be sent and summed in bfloat16 or wider, within the bound.
No kernel may reach another device: no remote copies, remote signals or barrier semaphores. Data moves between devices by JAX's collectives and lax.ppermute only.
A program may use at most 64 MiB of HBM per device.

v0:
```python
import math

import jax
import jax.numpy as jnp
from jax import lax
from jax.sharding import PartitionSpec as P

relaxation_scale_factor = 0.5
guarded_floor_entry = -1e30


def combined_all(part, axis, combine):
    gathered = jax.tree.map(lambda a: lax.all_gather(a, axis), part)

    def take(source):
        return jax.tree.map(lambda a: lax.dynamic_index_in_dim(a, source, 0, False), gathered)

    return lax.fori_loop(
        1, lax.axis_size(axis), lambda source, state: combine(state, take(source)), take(0)
    )


def from_behind(value, axis, steps):
    count = lax.axis_size(axis)
    pairs = [(source, (source + steps) % count) for source in range(count)]
    return lax.ppermute(value, axis, pairs)


def masked_logits(row_block, lone_document, live_image_embeddings):
    similarity_matrix = lax.dot_general(
        row_block, lone_document, (((1,), (1,)), ((), ())), preferred_element_type=jnp.float32
    )
    return jnp.where(
        live_image_embeddings[None, :] > 0,
        similarity_matrix / relaxation_scale_factor,
        guarded_floor_entry,
    )


def combine_parts(earlier, later):
    highest = jnp.maximum(earlier[0], later[0])
    totals = earlier[1] * jnp.exp(earlier[0] - highest) + later[1] * jnp.exp(later[0] - highest)
    return (highest, totals, earlier[2] + later[2])


def on_device(queries, query_mask, positive, page_vectors, page_mask):
    tokens = queries.shape[1]
    features = queries.shape[2]
    local_pages = page_vectors.shape[0]
    blocks = lax.axis_size("blk")
    members = lax.axis_size("group")
    bundle_size = queries.shape[0] * members
    total_queries = bundle_size * blocks
    natural_logarithm_lengths = jnp.log(jnp.sum(page_mask.astype(jnp.float32), axis=1))
    bundle_vectors, bundle_masks, bundle_targets = (
        lax.all_gather(queries, "group", axis=0, tiled=True),
        lax.all_gather(query_mask, "group", axis=0, tiled=True),
        lax.all_gather(positive, "group", axis=0, tiled=True),
    )

    def forward_piece(folded, shard_in, root_row):
        scores, lse_rows, live_all, owners, kept = folded
        vectors, token_masks, targets = shard_in
        amount = vectors.shape[0]
        stride = math.gcd(amount, max(1, 512 // tokens))

        def run_block(number, current):
            scores, lse_rows = current
            offset = number * stride
            slab_rows = lax.dynamic_slice_in_dim(vectors, offset, stride, 0).reshape(
                stride * tokens, features
            )
            alive = lax.dynamic_slice_in_dim(token_masks, offset, stride, 0).astype(jnp.float32)
            found_sums = []
            for index_page in range(local_pages):
                masked = masked_logits(slab_rows, page_vectors[index_page], page_mask[index_page])
                highest = jnp.max(masked, axis=1, keepdims=True)
                found_sums.append(
                    highest[:, 0] + jnp.log(jnp.sum(jnp.exp(masked - highest), axis=1))
                )
            logsumexp_results = jnp.stack(found_sums, axis=1).reshape(stride, tokens, local_pages)
            softened_supremum = relaxation_scale_factor * (
                logsumexp_results - natural_logarithm_lengths
            )
            page_score = jnp.sum(alive[:, :, None] * softened_supremum, axis=1)
            scores = lax.dynamic_update_slice_in_dim(scores, page_score, offset, 0)
            lse_rows = lax.dynamic_update_slice_in_dim(lse_rows, logsumexp_results, offset, 0)
            return (scores, lse_rows)

        scores, lse_rows = lax.fori_loop(0, amount // stride, run_block, (scores, lse_rows))
        live_all = lax.dynamic_update_slice_in_dim(live_all, token_masks, root_row, 0)
        owners = lax.dynamic_update_slice_in_dim(owners, targets, root_row, 0)
        kept = vectors
        return (scores, lse_rows, live_all, owners, kept)

    starting = (
        jnp.zeros((total_queries, local_pages), jnp.float32),
        jnp.zeros((total_queries, tokens, local_pages), jnp.float32),
        jnp.zeros((total_queries, tokens), jnp.int32),
        jnp.zeros((total_queries,), jnp.int32),
        jnp.zeros((total_queries, tokens, features), jnp.bfloat16),
    )
    scores, lse_rows, live_all, owners, kept = forward_piece(
        starting,
        (
            lax.all_gather(bundle_vectors, "blk", axis=0, tiled=True),
            lax.all_gather(bundle_masks, "blk", axis=0, tiled=True),
            lax.all_gather(bundle_targets, "blk", axis=0, tiled=True),
        ),
        jnp.int32(0),
    )
    position = lax.axis_index(("blk", "group"))
    page_ids = position * local_pages + jnp.arange(local_pages, dtype=jnp.int32)
    chosen = owners[:, None] == page_ids[None, :]
    picked_local = jnp.sum(jnp.where(chosen, scores, 0.0))
    local_top = jnp.max(scores, axis=1)
    local_total = jnp.sum(jnp.exp(scores - local_top[:, None]), axis=1)
    highest, totals, picked = combined_all(
        (local_top, local_total, picked_local), ("blk", "group"), combine_parts
    )
    page_lse = highest + jnp.log(totals)
    mean_loss = (jnp.sum(page_lse) - picked) / total_queries
    coefficient = jnp.exp(scores - page_lse[:, None]) - chosen.astype(jnp.float32)
    factor_scale = coefficient[:, None, :] * live_all.astype(jnp.float32)[:, :, None]

    def slice_rows(root_row, amount):
        sums = lax.dynamic_slice_in_dim(lse_rows, root_row, amount, 0).reshape(
            amount * tokens, local_pages
        )
        scales = lax.dynamic_slice_in_dim(factor_scale, root_row, amount, 0).reshape(
            amount * tokens, local_pages
        )
        return (sums, scales)

    def gradient_terms(row_block, logsumexp_results, scales, page_grads):
        partial_value = jnp.zeros(row_block.shape, jnp.float32)
        for number in range(local_pages):
            masked = masked_logits(row_block, page_vectors[number], page_mask[number])
            weights = jnp.exp(masked - logsumexp_results[:, number : number + 1])
            factor = (scales[:, number : number + 1] * weights).astype(jnp.bfloat16)
            partial_value = partial_value + jnp.dot(
                factor, page_vectors[number], preferred_element_type=jnp.float32
            )
            update = lax.dot_general(
                factor, row_block, (((0,), (0,)), ((), ())), preferred_element_type=jnp.float32
            )
            page_grads = page_grads.at[number].add(update)
        return (partial_value, page_grads)

    home = lax.axis_index("blk")
    page_grads = jnp.zeros(page_vectors.shape, jnp.float32)

    def visit_one(moving, collected, page_grads, lap_index):
        root_row = (home - lap_index) % blocks * bundle_size
        sums, scales = slice_rows(root_row, bundle_size)
        partial_value, page_grads = gradient_terms(
            moving.reshape(bundle_size * tokens, features), sums, scales, page_grads
        )
        return (collected + partial_value.reshape(bundle_size, tokens, features), page_grads)

    def pass_one(collected):
        return from_behind(collected, "blk", 1)

    def turn_one(lap_index, current):
        moving, collected, page_grads = current
        collected, page_grads = visit_one(moving, collected, page_grads, lap_index)
        moving = from_behind(moving, "blk", 1)
        return (moving, pass_one(collected), page_grads)

    empty_whole = jnp.zeros((bundle_size, tokens, features), jnp.float32)
    moving, collected, page_grads = lax.fori_loop(
        0, blocks - 1, turn_one, (bundle_vectors, empty_whole, page_grads)
    )
    collected, page_grads = visit_one(moving, collected, page_grads, blocks - 1)
    collected = pass_one(collected)
    grad_queries = lax.psum_scatter(collected, "group", scatter_dimension=0, tiled=True)
    return (grad_queries, page_grads, mean_loss)


def solution(mesh):
    in_specs = (
        P(("blk", "group"), None, None),
        P(("blk", "group"), None),
        P(("blk", "group")),
        P(("blk", "group"), None, None),
        P(("blk", "group"), None),
    )
    out_specs = (P(("blk", "group"), None, None), P(("blk", "group"), None, None), P())
    return jax.shard_map(
        on_device, mesh=mesh, in_specs=in_specs, out_specs=out_specs, check_vma=False
    )
```

profile of v0, /device:TPU:0, one launch (start us, length us, event | category | flops | bytes accessed | tf_op | source)
XLA Modules:
  0.0 262.9 jit_solution(15310981650806206361)
XLA Ops:
  7.2 0.8 compare_bitcast_fusion.2
  8.1 32.4 %all_gather.36 = bf16[8,16,128]{2,1,0:T(8,128)(2,1)S(1)} all-gather(bf16[1,16,128]{2,1,0:T(8,128)(2,1)S(1)} %copy-done.4), channel_id=1, replica_groups=mesh['blk'=4,'group'=8] {'group'}, dimensions={0}, use_global_device_ids=true | all-gather | bytes 36864 | tf_op jit(solution)/shard_map/all_gather | solution.py:56
  40.6 5.5 %all_gather.37 = bf16[32,16,128]{2,1,0:T(8,128)(2,1)S(1)} all-gather(bf16[8,16,128]{2,1,0:T(8,128)(2,1)S(1)} %all_gather.36), channel_id=1, replica_groups=mesh['blk'=4,'group'=8] {'blk'}, dimensions={0}, use_global_device_ids=true | all-gather | bytes 163840 | tf_op jit(solution)/shard_map/all_gather | solution.py:106
  46.8 0.7 copy-done.5
  47.5 20.4 %all-gather.2 = s32[8,1,16]{2,1,0:T(1,128)S(1)} all-gather(s32[1,1,16]{2,1,0:T(1,128)S(1)} %bitcast.182), channel_id=1, replica_groups=mesh['blk'=4,'group'=8] {'group'}, dimensions={0}, use_global_device_ids=true | all-gather | bytes 576 | tf_op jit(solution)/shard_map/all_gather | solution.py:57
  67.9 5.2 %all_gather.39 = s32[32,16]{1,0:T(8,128)S(1)} all-gather(s32[8,16]{1,0:T(8,128)S(1)} %bitcast.181), channel_id=1, replica_groups=mesh['blk'=4,'group'=8] {'blk'}, dimensions={0}, use_global_device_ids=true | all-gather | bytes 2560 | tf_op jit(solution)/shard_map/all_gather | solution.py:107
  73.1 0.7 copy-done.7
  75.0 0.8 dynamic-update-slice.28
  75.8 6.8 %all-reduce.2 = s32[8]{0:T(128)S(1)} all-reduce(s32[8]{0:T(128)S(1)} %dynamic-update-slice.28), channel_id=1, replica_groups=mesh['blk'=4,'group'=8] {'group'}, use_global_device_ids=true, to_apply=%add.2 | all-reduce | flops 8 | bytes 64
  84.1 4.9 %all-reduce.3 = s32[32]{0:T(128)S(1)} all-reduce(s32[32]{0:T(128)S(1)} %dynamic-update-slice.29), channel_id=1, replica_groups=mesh['blk'=4,'group'=8] {'blk'}, use_global_device_ids=true, to_apply=%add.3 | all-reduce | flops 32 | bytes 256
  89.2 0.7 fusion.54
  90.3 0.8 dynamic-update-slice.30
  91.0 40.5 %all-reduce.5 = (f32[1024]{0:T(1024)S(1)}, f32[1024]{0:T(1024)S(1)}, f32[32]{0:T(128)S(1)}) all-reduce(f32[1024]{0:T(1024)S(1)} %dynamic-update-slice.26, f32[1024]{0:T(1024)S(1)} %dynamic-update-slice.27, f32[32]{0:T(128)S(1)} %dynamic-update-slice.30), channel_id=2, replica_groups=mesh['blk'=4,'group'=8] {'blk','group'}, use_global_device_ids=true, to_apply=%add | all-reduce | flops 2080 | bytes 16640
  131.7 39.9 %while.48 = (s32[]{:T(128)}, f32[32]{0:T(128)S(1)}, f32[32]{0:T(128)S(1)}, f32[]{:T(128)}, f32[32,32]{1,0:T(8,128)S(1)}, /*index=5*/f32[32,32]{1,0:T(8,128)S(1)}, f32[32]{0:T(128)S(1)}, s32[]{:T(128)}, s32[]{:T(128)}, s32[]{:T(128)}) while((s32[]{:T(128)}, f32[32]{0:T(128)S(1)}, f32[32]{0:T(128)S(1)}, f32[]{:T(128)}, ...), condition=%wide.region_10.11_spmd, body=%wide.region_9.10_spmd.sunk | while | flops 198 | bytes 939 | solution.py:18
  172.6 13.9 %while.49 = (s32[]{:T(128)}, bf16[8,16,128]{2,1,0:T(8,128)(2,1)S(1)}, f32[8,16,128]{2,1,0:T(8,128)S(1)}, f32[2,128,128]{2,1,0:T(8,128)S(1)}, s32[]{:T(128)}, /*i...) while((s32[]{:T(128)}, ...), condition=%wide.region_12.13_spmd, body=%wide.region_11.12_spmd.sunk | while | flops 25395472 | bytes 1589896 | solution.py:171
  173.6 2.4 collective-permute-start.1
  176.4 0.9 collective-permute-done.1
  178.2 2.4 collective-permute-start.1
  181.0 0.9 collective-permute-done.1
  182.8 2.4 collective-permute-start.1
  185.6 0.9 collective-permute-done.1
  188.1 2.8 %collective-permute-done.2 = f32[8,16,128]{2,1,0:T(8,128)S(1)} collective-permute-done((f32[8,16,128]{2,1,0:T(8,128)S(1)}, f32[8,16,128]{2,1,0:T(8,128)S(1)}, u32[]{:S(2)}, u32[]{:S(2)}) %collective-permute-start.2) | collective-permute-done | bytes 65568 | tf_op jit(solution)/shard_map/ppermute | solution.py:26
  190.9 0.6 copy-done.2
  191.8 63.1 %reduce-scatter.2.cloned.1.call-done = f32[1,16,128]{2,1,0:T(8,128)} async-done(((f32[8,16,128]{2,1,0:T(8,128)}), f32[1,16,128]{2,1,0:T(8,128)}) %reduce-scatter.2.cloned.1.call-update) | async-done | bytes 8208 | tf_op jit(solution)/shard_map/reduce_scatter | solution.py:176
  (174 shorter events, 27.7 us)
Async XLA Ops:
  7.2 0.8 copy-start.3
  7.2 0.9 copy-start.4
  7.2 247.7 %reduce-scatter.2.cloned.1.call-start = ((), (), s32[]{:S(2)}) async-start(), calls=%async_computation.1 | async-start | bytes 73728 | tf_op jit(solution)/shard_map/reduce_scatter | solution.py:176
  40.5 5.5 %copy-start.1 = (bf16[2,128,128]{2,1,0:T(8,128)(2,1)S(1)}, bf16[2,128,128]{2,1,0:T(8,128)(2,1)}, u32[]{:S(2)}) copy-start(bf16[2,128,128]{2,1,0:T(8,128)(2,1)} %param.20) | copy-start | bytes 196612
  46.8 0.7 copy-start.5
  73.1 0.7 copy-start.7
  75.8 6.8 %copy-start.6 = (u32[32]{0:T(128)S(1)}, u32[32]{0:T(128)}, u32[]{:S(2)}) copy-start(u32[32]{0:T(128)} %constant.385) | copy-start | bytes 388
  172.6 3.7 %collective-permute-start = (bf16[8,16,128]{2,1,0:T(8,128)(2,1)S(1)}, bf16[8,16,128]{2,1,0:T(8,128)(2,1)S(1)}, u32[]{:S(2)}, u32[]{:S(2)}) collective-permute-start(bf16[8,16,128]{2,1,0:T(8,128)(2,1)S(1)} %copy.33), channel_id=1, source_target_pairs={{0,8},{8,16},{16,24},{24,0},{1,9},{9,17},{17,25},{25,1},{2,10},{10... | collective-permute-start | bytes 98312 | tf_op jit(solution)/shard_map/while/body/eval_jaxpr/ppermute | solution.py:26
  173.6 3.7 %collective-permute-start.1 = (f32[8,16,128]{2,1,0:T(8,128)S(1)}, f32[8,16,128]{2,1,0:T(8,128)S(1)}, u32[]{:S(2)}, u32[]{:S(2)}) collective-permute-start(f32[8,16,128]{2,1,0:T(8,128)S(1)} %add.305), channel_id=1, source_target_pairs={{0,8},{8,16},{16,24},{24,0},{1,9},{9,17},{17,25},{25,1},{2,10},{10... | collective-permute-start | bytes 196616 | tf_op jit(solution)/shard_map/while/body/eval_jaxpr/ppermute | solution.py:26
  177.3 3.7 %collective-permute-start = (bf16[8,16,128]{2,1,0:T(8,128)(2,1)S(1)}, bf16[8,16,128]{2,1,0:T(8,128)(2,1)S(1)}, u32[]{:S(2)}, u32[]{:S(2)}) collective-permute-start(bf16[8,16,128]{2,1,0:T(8,128)(2,1)S(1)} %copy.33), channel_id=1, source_target_pairs={{0,8},{8,16},{16,24},{24,0},{1,9},{9,17},{17,25},{25,1},{2,10},{10... | collective-permute-start | bytes 98312 | tf_op jit(solution)/shard_map/while/body/eval_jaxpr/ppermute | solution.py:26
  178.2 3.7 %collective-permute-start.1 = (f32[8,16,128]{2,1,0:T(8,128)S(1)}, f32[8,16,128]{2,1,0:T(8,128)S(1)}, u32[]{:S(2)}, u32[]{:S(2)}) collective-permute-start(f32[8,16,128]{2,1,0:T(8,128)S(1)} %add.305), channel_id=1, source_target_pairs={{0,8},{8,16},{16,24},{24,0},{1,9},{9,17},{17,25},{25,1},{2,10},{10... | collective-permute-start | bytes 196616 | tf_op jit(solution)/shard_map/while/body/eval_jaxpr/ppermute | solution.py:26
  182.0 3.6 %collective-permute-start = (bf16[8,16,128]{2,1,0:T(8,128)(2,1)S(1)}, bf16[8,16,128]{2,1,0:T(8,128)(2,1)S(1)}, u32[]{:S(2)}, u32[]{:S(2)}) collective-permute-start(bf16[8,16,128]{2,1,0:T(8,128)(2,1)S(1)} %copy.33), channel_id=1, source_target_pairs={{0,8},{8,16},{16,24},{24,0},{1,9},{9,17},{17,25},{25,1},{2,10},{10... | collective-permute-start | bytes 98312 | tf_op jit(solution)/shard_map/while/body/eval_jaxpr/ppermute | solution.py:26
  182.8 3.7 %collective-permute-start.1 = (f32[8,16,128]{2,1,0:T(8,128)S(1)}, f32[8,16,128]{2,1,0:T(8,128)S(1)}, u32[]{:S(2)}, u32[]{:S(2)}) collective-permute-start(f32[8,16,128]{2,1,0:T(8,128)S(1)} %add.305), channel_id=1, source_target_pairs={{0,8},{8,16},{16,24},{24,0},{1,9},{9,17},{17,25},{25,1},{2,10},{10... | collective-permute-start | bytes 196616 | tf_op jit(solution)/shard_map/while/body/eval_jaxpr/ppermute | solution.py:26
  187.2 3.7 %collective-permute-start.2 = (f32[8,16,128]{2,1,0:T(8,128)S(1)}, f32[8,16,128]{2,1,0:T(8,128)S(1)}, u32[]{:S(2)}, u32[]{:S(2)}) collective-permute-start(f32[8,16,128]{2,1,0:T(8,128)S(1)} %add.250), channel_id=1, source_target_pairs={{0,8},{8,16},{16,24},{24,0},{1,9},{9,17},{17,25},{25,1},{2,10},{10... | collective-permute-start | bytes 196616 | tf_op jit(solution)/shard_map/ppermute | solution.py:26
  190.9 0.6 copy-start.2
  191.8 63.1 %copy-start = (f32[2,128,128]{2,1,0:T(8,128)}, f32[2,128,128]{2,1,0:T(8,128)S(1)}, u32[]{:S(2)}) copy-start(f32[2,128,128]{2,1,0:T(8,128)S(1)} %fusion.38) | copy-start | bytes 393220
Sparse Core Ops, SparseCore 0:
  191.7 63.1 reduce-scatter.1
where the time goes:
time: 264 us; the launch traced here: 263 us
  blocking collectives  116 us (44%)
  waiting for transfers between devices  68.8 us (26%)
  local copies, waits for them, and re-layouts  24.5 us (9%)
  loops' own time  21.1 us (8%)
  between operations  17.3 us (7%)
  starting transfers between devices  7.44 us (3%)
  matrix products  4.3 us (2%)
  other arithmetic  3.58 us (1%)
    reduce_scatter x1, waiting for transfers between devices, on_device(): lax.psum_scatter(collected, 'group', scatter_dimension=0, tiled=True)  63.1 us
    unnamed x3, blocking collectives  52.2 us
    all_gather x1, blocking collectives, on_device(): lax.all_gather(queries, 'group', axis=0, tiled=True)  32.4 us
    another operation x1, loops' own time, combined_all(): lax.fori_loop(1, lax.axis_size(axis), lambda source, state: combine(state...  20.9 us
    all_gather x1, blocking collectives, on_device(): lax.all_gather(query_mask, 'group', axis=0, tiled=True)  20.4 us
    dynamic_slice x33, local copies, waits for them, and re-layouts, take(): lax.dynamic_index_in_dim(a, source, 0, False)  18.2 us
    ppermute x7, starting transfers between devices, from_behind(): return lax.ppermute(value, axis, pairs)  7.4 us
    ppermute x7, waiting for transfers between devices, from_behind(): return lax.ppermute(value, axis, pairs)  5.66 us
  transfers between devices with their start and end apart: 8, of which 5 were waited for; matrix products, arithmetic and copies ran while one was open for 1% of the time, Pallas kernels for 0%

commit v1 on v0

--- a/solution.py
+++ b/solution.py
@@ -1,8 +1,11 @@
+import functools
 import math
 
 import jax
 import jax.numpy as jnp
 from jax import lax
+from jax.experimental import pallas as pl
+from jax.experimental.pallas import tpu as pltpu
 from jax.sharding import PartitionSpec as P
 
 relaxation_scale_factor = 0.5
@@ -43,7 +46,7 @@
     return (highest, totals, earlier[2] + later[2])
 
 
-def on_device(queries, query_mask, positive, page_vectors, page_mask):
+def general_path(queries, query_mask, positive, page_vectors, page_mask):
     tokens = queries.shape[1]
     features = queries.shape[2]
     local_pages = page_vectors.shape[0]
@@ -177,6 +180,236 @@
     return (grad_queries, page_grads, mean_loss)
 
 
+LANES = 128
+EXTRA = 8
+
+
+def fits(queries, page_vectors, devices):
+    tokens, features = queries.shape[1:]
+    lanes = devices * tokens
+    return (
+        queries.shape[0] == 1
+        and tokens % 8 == 0
+        and LANES % tokens == 0
+        and features == LANES
+        and page_vectors.shape[1] == LANES
+        and lanes % LANES == 0
+        and 2 * (lanes // LANES) <= EXTRA
+        and lax.axis_size("blk") % 2 == 0
+    )
+
+
+def segment_sum(values, width):
+    lanes = values.shape[1]
+    lane = lax.broadcasted_iota(jnp.int32, values.shape, 1)
+    step = 1
+    while step < width:
+        ahead = pltpu.roll(values, lanes - step, 1)
+        behind = pltpu.roll(values, step, 1)
+        values = values + jnp.where((lane & step) == 0, ahead, behind)
+        step *= 2
+    return values
+
+
+def split_half(value):
+    scaled = value * 8193.0
+    high = scaled - (scaled - value)
+    return high, value - high
+
+
+def middle_kernel(tokens, sent_ref, own_ref, other_ref, own_mask_ref, other_mask_ref, out_ref, weight_ref, stat_ref):
+    sources = sent_ref.shape[0]
+    lanes = sources * tokens
+    chunks = lanes // LANES
+    per_chunk = LANES // tokens
+    local_pages = own_ref.shape[0]
+    blk = lax.axis_index("blk")
+    group = lax.axis_index("group")
+    members = lax.axis_size("group")
+    bases = [
+        (blk * members + group) * local_pages,
+        ((blk ^ 1) * members + group) * local_pages,
+    ]
+
+    extra = sent_ref[:, tokens : tokens + EXTRA, :].astype(jnp.float32)
+    slot = lax.broadcasted_iota(jnp.int32, (EXTRA, LANES), 1) // tokens
+    rows = []
+    for chunk in range(chunks):
+        total = jnp.zeros((EXTRA, LANES), jnp.float32)
+        for i in range(per_chunk):
+            total = jnp.where(slot == i, extra[chunk * per_chunk + i], total)
+        rows.append(total)
+    rows = jnp.concatenate(rows, axis=1)
+    alive = rows[0:1]
+    target = (rows[1:2] * 256.0 + rows[2:3]).astype(jnp.int32)
+
+    rows_q = sent_ref[:, 0:tokens, :].reshape(lanes, LANES)
+    patch = lax.broadcasted_iota(jnp.int32, (LANES, lanes), 0).astype(jnp.float32)
+    tokens_soft, weights, ids = [], [], []
+    for vectors_ref, mask_ref, base in (
+        (own_ref, own_mask_ref, bases[0]),
+        (other_ref, other_mask_ref, bases[1]),
+    ):
+        for number in range(local_pages):
+            count = jnp.sum(mask_ref[number : number + 1, :].astype(jnp.float32), axis=1, keepdims=True)
+            similarity = lax.dot_general(
+                vectors_ref[number], rows_q, (((1,), (1,)), ((), ())), preferred_element_type=jnp.float32
+            )
+            masked = jnp.where(patch < count, similarity / relaxation_scale_factor, guarded_floor_entry)
+            highest = jnp.max(masked, axis=0, keepdims=True)
+            powers = jnp.exp(masked - highest)
+            total = jnp.sum(powers, axis=0, keepdims=True)
+            lse = highest + jnp.log(total)
+            tokens_soft.append(alive * (relaxation_scale_factor * (lse - jnp.log(count))))
+            weights.append(powers * (1.0 / total))
+            ids.append(base + number)
+    scores = segment_sum(jnp.concatenate(tokens_soft, axis=0), tokens)
+    top = jnp.max(scores, axis=0, keepdims=True)
+    chip_lse = top + jnp.log(jnp.sum(jnp.exp(scores - top), axis=0, keepdims=True))
+
+    sends_sum = (blk & 1) == 0
+    picked = jnp.zeros((1, lanes), jnp.float32)
+    high_terms, low_terms = [], []
+    for number in range(2 * local_pages):
+        score = scores[number : number + 1]
+        hit = target == ids[number]
+        picked = picked + jnp.where(hit, score, 0.0)
+        scale = alive * jnp.where(sends_sum, jnp.exp(score - chip_lse), hit.astype(jnp.float32))
+        term = weights[number] * scale
+        high = term.astype(jnp.bfloat16)
+        high_terms.append(high)
+        low_terms.append((term - high.astype(jnp.float32)).astype(jnp.bfloat16))
+    vectors = jnp.concatenate([own_ref[...], other_ref[...]], axis=0).reshape(2 * local_pages * LANES, LANES)
+    contract = (((0,), (0,)), ((), ()))
+    mixed = lax.dot_general(
+        vectors, jnp.concatenate(high_terms, axis=0), contract, preferred_element_type=jnp.float32
+    ) + lax.dot_general(
+        vectors, jnp.concatenate(low_terms, axis=0), contract, preferred_element_type=jnp.float32
+    )
+    out_ref[:, 0:tokens, :] = mixed.T.reshape(sources, tokens, LANES)
+    high, low = split_half(jnp.where(sends_sum, chip_lse, picked))
+    pieces = [high[:, c * LANES : (c + 1) * LANES] for c in range(chunks)]
+    pieces += [jnp.zeros((1, LANES), jnp.float32)] * (EXTRA // 2 - chunks)
+    pieces += [low[:, c * LANES : (c + 1) * LANES] for c in range(chunks)]
+    pieces += [jnp.zeros((1, LANES), jnp.float32)] * (EXTRA // 2 - chunks)
+    out_ref[:, tokens : tokens + EXTRA, :] = jnp.broadcast_to(
+        jnp.concatenate(pieces, axis=0)[None], (sources, EXTRA, LANES)
+    )
+    for number in range(local_pages):
+        weight_ref[number] = weights[number] * alive
+        stat_ref[number : number + 1, :] = scores[number : number + 1]
+        stat_ref[local_pages + number : local_pages + number + 1, :] = (target == ids[number]).astype(jnp.float32)
+
+
+def last_kernel(tokens, got_ref, sent_ref, weight_ref, stat_ref, grad_q_ref, grad_p_ref, loss_ref):
+    sources = sent_ref.shape[0]
+    lanes = sources * tokens
+    chunks = lanes // LANES
+    local_pages = weight_ref.shape[0]
+    blk = lax.axis_index("blk")
+    group = lax.axis_index("group")
+    members = lax.axis_size("group")
+    me = blk * members + group
+    even = [s for s in range(sources) if (s // members) % 2 == 0]
+    odd = [s for s in range(sources) if (s // members) % 2 == 1]
+
+    def stats(source):
+        rows = got_ref[source, tokens : tokens + EXTRA, :]
+        return rows + pltpu.roll(rows, EXTRA // 2, 0)
+
+    chip_lse = [stats(s) for s in even]
+    top = functools.reduce(jnp.maximum, chip_lse)
+    page_lse = top + jnp.log(sum(jnp.exp(c - top) for c in chip_lse))
+    picked = sum(stats(s) for s in odd)
+    row = lax.broadcasted_iota(jnp.int32, (EXTRA, LANES), 0)
+    lane = lax.broadcasted_iota(jnp.int32, (EXTRA, LANES), 1)
+    difference = jnp.where(row < chunks, page_lse - picked, 0.0)
+    loss_ref[...] = jnp.sum(
+        jnp.sum(difference, axis=0, keepdims=True), axis=1, keepdims=True
+    ) * (1.0 / (tokens * sources))
+
+    mine = (row == me * tokens // LANES) & (lane == me * tokens % LANES)
+    ratios = jnp.concatenate(
+        [
+            jnp.sum(jnp.where(mine, jnp.exp(c - page_lse), 0.0), axis=0, keepdims=True)
+            for c in chip_lse
+        ],
+        axis=0,
+    )
+    ratios = jnp.broadcast_to(jnp.sum(ratios, axis=1, keepdims=True), ratios.shape)
+    grad_q = jnp.zeros((tokens, LANES), jnp.float32)
+    for i, s in enumerate(even):
+        grad_q = grad_q + ratios[i : i + 1, :] * got_ref[s, 0:tokens, :]
+    for s in odd:
+        grad_q = grad_q - got_ref[s, 0:tokens, :]
+    grad_q_ref[0] = grad_q
+
+    flat = jnp.concatenate([page_lse[c : c + 1] for c in range(chunks)], axis=1)
+    rows_q = sent_ref[:, 0:tokens, :].reshape(lanes, LANES)
+    for number in range(local_pages):
+        coefficient = (
+            jnp.exp(stat_ref[number : number + 1, :] - flat)
+            - stat_ref[local_pages + number : local_pages + number + 1, :]
+        )
+        factor = (coefficient * weight_ref[number]).astype(jnp.bfloat16)
+        grad_p_ref[number] = jnp.dot(factor, rows_q, preferred_element_type=jnp.float32)
+
+
+def exchange(blocks_to_all):
+    return lax.all_to_all(blocks_to_all, ("blk", "group"), 0, 0, tiled=True)
+
+
+def two_exchanges(queries, query_mask, positive, page_vectors, page_mask):
+    tokens = queries.shape[1]
+    local_pages = page_vectors.shape[0]
+    devices = lax.axis_size("blk") * lax.axis_size("group")
+    lanes = devices * tokens
+    blocks = lax.axis_size("blk")
+    swap = [(b, b ^ 1) for b in range(blocks)]
+    other_vectors = lax.ppermute(page_vectors, "blk", swap)
+    other_mask = lax.ppermute(page_mask, "blk", swap)
+
+    kind = lax.broadcasted_iota(jnp.int32, (1, EXTRA, LANES), 1)
+    number = positive[:, None, None]
+    extra = jnp.where(
+        kind == 0,
+        jnp.tile(query_mask, (1, LANES // tokens))[:, None, :],
+        jnp.where(kind == 1, number // 256, number % 256),
+    ).astype(jnp.bfloat16)
+    message = jnp.concatenate([queries, extra], axis=1)
+    sent = exchange(jnp.broadcast_to(message, (devices, tokens + EXTRA, LANES)))
+
+    vmem = pl.BlockSpec(memory_space=pltpu.VMEM)
+    out, weights, stats = pl.pallas_call(
+        functools.partial(middle_kernel, tokens),
+        out_shape=(
+            jax.ShapeDtypeStruct((devices, tokens + EXTRA, LANES), jnp.float32),
+            jax.ShapeDtypeStruct((local_pages, LANES, lanes), jnp.float32),
+            jax.ShapeDtypeStruct((2 * local_pages, lanes), jnp.float32),
+        ),
+        in_specs=[vmem] * 5,
+        out_specs=(vmem, vmem, vmem),
+    )(sent, page_vectors, other_vectors, page_mask, other_mask)
+    got = exchange(out.astype(jnp.float16)).astype(jnp.float32)
+    grad_q, grad_p, loss = pl.pallas_call(
+        functools.partial(last_kernel, tokens),
+        out_shape=(
+            jax.ShapeDtypeStruct(queries.shape, jnp.float32),
+            jax.ShapeDtypeStruct(page_vectors.shape, jnp.float32),
+            jax.ShapeDtypeStruct((1, 1), jnp.float32),
+        ),
+        in_specs=[vmem] * 4,
+        out_specs=(vmem, vmem, vmem),
+    )(got, sent, weights, stats)
+    return (grad_q, grad_p, loss[0, 0])
+
+
+def on_device(queries, query_mask, positive, page_vectors, page_mask):
+    devices = lax.axis_size("blk") * lax.axis_size("group")
+    chosen = two_exchanges if fits(queries, page_vectors, devices) else general_path
+    return chosen(queries, query_mask, positive, page_vectors, page_mask)
+
+
 def solution(mesh):
     in_specs = (
         P(("blk", "group"), None, None),

time: 264 us -> 38.6 us (0.15)
  blocking collectives: 116 us -> 11.4 us
  waiting for transfers between devices: 68.8 us -> 7.67 us
  local copies, waits for them, and re-layouts: 24.5 us -> 2.74 us
  loops' own time: 21.1 us -> 0 us
  between operations: 17.3 us -> 1.36 us
  Pallas kernels: 0 us -> 5.27 us
  matrix products: 4.3 us -> 0 us
    all_gather x4 -> x0, blocking collectives: 63.6 us -> none  [the longest x1 32.4 us: on_device(): lax.all_gather(queries, 'group', axis=0, tiled=True)]
    reduce_scatter x1 -> x0, waiting for transfers between devices: 63.1 us -> none  [on_device(): lax.psum_scatter(collected, 'group', scatter_dimension=0, tiled=True)]
    unnamed x3 -> x0, blocking collectives: 52.2 us -> none
    another operation x2 -> x0, loops' own time: 21.1 us -> none  [the longest x1 20.9 us: combined_all(): lax.fori_loop(1, lax.axis_size(axis), lambda source, state: combine(state...]
    dynamic_slice x37 -> x0, local copies, waits for them, and re-layouts: 18.2 us -> none  [the longest x33 18.2 us: take(): lax.dynamic_index_in_dim(a, source, 0, False)]
    all_to_all x0 -> x1, blocking collectives: none -> 11.4 us  [exchange(): return lax.all_to_all(blocks_to_all, ('blk', 'group'), 0, 0, tiled=True)]
    all_to_all x0 -> x1, starting transfers between devices: none -> 7.33 us  [exchange(): return lax.all_to_all(blocks_to_all, ('blk', 'group'), 0, 0, tiled=True)]
    ppermute x7 -> x2, starting transfers between devices: 7.4 us -> 0.58 us  [the longest x1 0.32 us: two_exchanges(): other_vectors = lax.ppermute(page_vectors, 'blk', swap)]
  transfers between devices with their start and end apart: 8 -> 3, of which waited for: 5 -> 2; matrix products, arithmetic and copies ran while one was open for 1% -> 0% of each run, Pallas kernels for 0% -> 0%
where the time goes in v1:
time: 38.6 us; the launch traced here: 38.2 us
  blocking collectives  11.4 us (30%)
  starting transfers between devices  7.9 us (20%)
  waiting for transfers between devices  7.67 us (20%)
  Pallas kernels  5.27 us (14%)
  local copies, waits for them, and re-layouts  2.74 us (7%)
  other arithmetic  1.88 us (5%)
  between operations  1.36 us (4%)
    all_to_all x1, blocking collectives, exchange(): return lax.all_to_all(blocks_to_all, ('blk', 'group'), 0, 0, tiled=True)  11.4 us
    all_to_all x1, starting transfers between devices, exchange(): return lax.all_to_all(blocks_to_all, ('blk', 'group'), 0, 0, tiled=True)  7.33 us
    all_to_all x1, waiting for transfers between devices, exchange(): return lax.all_to_all(blocks_to_all, ('blk', 'group'), 0, 0, tiled=True)  6.76 us
    pallas_call x1, Pallas kernels, two_exchanges(): pl.pallas_call(functools.partial(middle_kernel, tokens), out_shape=(jax.S...  3.06 us
    pallas_call x1, Pallas kernels, two_exchanges(): pl.pallas_call(functools.partial(last_kernel, tokens), out_shape=(jax.Sha...  2.21 us
    unnamed x14, local copies, waits for them, and re-layouts  1.95 us
    convert_element_type x2, other arithmetic, two_exchanges(): got = exchange(out.astype(jnp.float16)).astype(jnp.float32)  1.79 us
    ppermute x1, waiting for transfers between devices, two_exchanges(): other_mask = lax.ppermute(page_mask, 'blk', swap)  0.9 us
  transfers between devices with their start and end apart: 3, of which 2 were waited for; matrix products, arithmetic and copies ran while one was open for 0% of the time, Pallas kernels for 0%

profile of v1, /device:TPU:0, one launch (start us, length us, event | category | flops | bytes accessed | tf_op | source)
XLA Modules:
  0.0 38.2 jit_solution(4392348636106363881)
XLA Ops:
  1.3 0.0 copy-start.6
  1.3 0.6 %copy-done.6 = s32[1,16]{1,0:T(1,128)S(1)} copy-done((s32[1,16]{1,0:T(1,128)S(1)}, s32[1,16]{1,0:T(1,128)}, u32[]{:S(2)}) %copy-start.6) | copy-done | bytes 88
  2.0 0.1 broadcast_in_dim.40
  2.1 0.0 copy-start.3
  2.1 0.1 select_convert_fusion
  2.2 0.6 %copy-done.3 = bf16[1,16,128]{2,1,0:T(8,128)(2,1)S(1)} copy-done((bf16[1,16,128]{2,1,0:T(8,128)(2,1)S(1)}, bf16[1,16,128]{2,1,0:T(8,128)(2,1)}, u32[]{:S(2)}) %copy-start.3) | copy-done | bytes 4120
  2.8 0.7 %broadcast_in_dim.48 = bf16[32,24,128]{2,1,0:T(8,128)(2,1)} broadcast(bf16[24,128]{1,0:T(8,128)(2,1)S(1)} %maximum_bitcast_fusion), dimensions={1,2} | broadcast | bytes 202752 | tf_op jit(solution)/shard_map/broadcast_in_dim | solution.py:380
  3.5 0.0 copy-start.1
  3.5 7.3 %all-to-all-start = ((bf16[32,24,128]{2,1,0:T(8,128)(2,1)}), bf16[32,24,128]{2,1,0:T(8,128)(2,1)S(1)}, u32[]{:S(2)}, u32[]{:S(2)}) async-start(bf16[32,24,128]{2,1,0:T(8,128)(2,1)} %broadcast_in_dim.48), calls=%async_computation | async-start | bytes 393216 | tf_op jit(solution)/shard_map/all_to_all | solution.py:359
  10.8 0.0 copy-done.1
  10.8 0.3 collective-permute-start
  11.1 0.0 copy-done.4
  11.1 0.3 collective-permute-start.1
  11.4 0.9 %collective-permute-done.1.other_mask_ref = s32[2,128]{1,0:T(2,128)S(1)} collective-permute-done((s32[2,128]{1,0:T(2,128)S(1)}, s32[2,128]{1,0:T(2,128)S(1)}, u32[]{:S(2)}, u32[]{:S(2)}) %collective-permute-start.1) | collective-permute-done | bytes 1056 | tf_op jit(solution)/shard_map/ppermute | solution.py:370
  12.3 0.0 collective-permute-done.other_ref
  12.3 6.8 %all-to-all-done.sent_ref = bf16[32,24,128]{2,1,0:T(8,128)(2,1)S(1)} async-done(((bf16[32,24,128]{2,1,0:T(8,128)(2,1)}), bf16[32,24,128]{2,1,0:T(8,128)(2,1)S(1)}, u32[]{:S(2)}, u32[]{:S(2)}) %all-to-all-start) | async-done | bytes 196640 | tf_op jit(solution)/shard_map/all_to_all | solution.py:359
  19.1 0.0 copy-done.5
  19.1 0.0 copy-done.2
  19.1 0.7 %copy-done = bf16[32,24,128]{2,1,0:T(8,128)(2,1)} copy-done((bf16[32,24,128]{2,1,0:T(8,128)(2,1)}, bf16[32,24,128]{2,1,0:T(8,128)(2,1)S(1)}, u32[]{:S(2)}) %copy-start) | copy-done | bytes 196632
  19.8 3.1 %shard_map.76 = (f32[32,24,128]{2,1,0:T(8,128)}, f32[2,128,512]{2,1,0:T(8,128)}, f32[4,512]{1,0:T(4,128)}) custom-call(bf16[32,24,128]{2,1,0:T(8,128)(2,1)} %copy-done, bf16[2,128,128]{2,1,0:T(8,128)(2,1)} %own_ref.1, bf16[2,128,128]{2,1,0:T(8,128)(2,1)} %copy-done.2, s32[2,128]{1,0:T(2,128)} %own_mask_ref.1, s32[2,128]{1,0:T(2,128)} %copy-done.5), custom_call_target="tpu_custom_call" | custom-call | tf_op jit(solution)/shard_map/pallas_call | solution.py:383
  22.8 1.0 %convert_element_type.18 = f16[32,24,128]{2,1,0:T(8,128)(2,1)S(1)} convert(f32[32,24,128]{2,1,0:T(8,128)} %get-tuple-element.9) | non-fusion elementwise | flops 98304 | bytes 589824 | tf_op jit(solution)/shard_map/convert_element_type | solution.py:393
  23.8 11.4 %all_to_all.10 = f16[32,24,128]{2,1,0:T(8,128)(2,1)S(1)} all-to-all(f16[32,24,128]{2,1,0:T(8,128)(2,1)S(1)} %convert_element_type.18), channel_id=1, replica_groups=mesh['blk'=4,'group'=8] {'blk','group'}, dimensions={0} | all-to-all | bytes 393216 | tf_op jit(solution)/shard_map/all_to_all | solution.py:359
  35.2 0.8 %convert_element_type.19.got_ref = f32[32,24,128]{2,1,0:T(8,128)} convert(f16[32,24,128]{2,1,0:T(8,128)(2,1)S(1)} %all_to_all.10) | non-fusion elementwise | flops 98304 | bytes 589824 | tf_op jit(solution)/shard_map/convert_element_type | solution.py:393
  36.0 2.2 %shard_map.77 = (f32[1,16,128]{2,1,0:T(8,128)}, f32[2,128,128]{2,1,0:T(8,128)}, f32[1,1]{1,0:T(1,128)}) custom-call(f32[32,24,128]{2,1,0:T(8,128)} %convert_element_type.19.got_ref, bf16[32,24,128]{2,1,0:T(8,128)(2,1)} %copy-done, f32[2,128,512]{2,1,0:T(8,128)} %get-tuple-element.10.weight_ref, f32[4,512]{1,0:T(4,128)} %get-tuple-element.11.stat_ref), custom_call_target="tpu_custom_call" | custom-call | tf_op jit(solution)/shard_map/pallas_call | solution.py:394
  (8 shorter events, 0.0 us)
Async XLA Ops:
  1.3 0.7 %copy-start.6 = (s32[1,16]{1,0:T(1,128)S(1)}, s32[1,16]{1,0:T(1,128)}, u32[]{:S(2)}) copy-start(s32[1,16]{1,0:T(1,128)} %param.6) | copy-start | bytes 196
  2.1 0.7 %copy-start.3 = (bf16[1,16,128]{2,1,0:T(8,128)(2,1)S(1)}, bf16[1,16,128]{2,1,0:T(8,128)(2,1)}, u32[]{:S(2)}) copy-start(bf16[1,16,128]{2,1,0:T(8,128)(2,1)} %param.5) | copy-start | bytes 12292
  3.5 7.3 %copy-start.1 = (bf16[2,128,128]{2,1,0:T(8,128)(2,1)S(1)}, bf16[2,128,128]{2,1,0:T(8,128)(2,1)}, u32[]{:S(2)}) copy-start(bf16[2,128,128]{2,1,0:T(8,128)(2,1)} %own_ref.1) | copy-start | bytes 196612
  3.5 7.7 %copy-start.4 = (s32[2,128]{1,0:T(2,128)S(1)}, s32[2,128]{1,0:T(2,128)}, u32[]{:S(2)}) copy-start(s32[2,128]{1,0:T(2,128)} %own_mask_ref.1) | copy-start | bytes 3076
  3.5 15.6 %all-to-all-start = ((bf16[32,24,128]{2,1,0:T(8,128)(2,1)}), bf16[32,24,128]{2,1,0:T(8,128)(2,1)S(1)}, u32[]{:S(2)}, u32[]{:S(2)}) async-start(bf16[32,24,128]{2,1,0:T(8,128)(2,1)} %broadcast_in_dim.48), calls=%async_computation | async-start | bytes 393216 | tf_op jit(solution)/shard_map/all_to_all | solution.py:359
  10.8 1.5 %collective-permute-start = (bf16[2,128,128]{2,1,0:T(8,128)(2,1)S(1)}, bf16[2,128,128]{2,1,0:T(8,128)(2,1)S(1)}, u32[]{:S(2)}, u32[]{:S(2)}) collective-permute-start(bf16[2,128,128]{2,1,0:T(8,128)(2,1)S(1)} %copy-done.1), channel_id=1, source_target_pairs={{0,8},{8,0},{16,24},{24,16},{1,9},{9,1},{17,25},{25,17},{2,10},{10... | collective-permute-start | bytes 196616 | tf_op jit(solution)/shard_map/ppermute | solution.py:369
  11.1 1.2 %collective-permute-start.1 = (s32[2,128]{1,0:T(2,128)S(1)}, s32[2,128]{1,0:T(2,128)S(1)}, u32[]{:S(2)}, u32[]{:S(2)}) collective-permute-start(s32[2,128]{1,0:T(2,128)S(1)} %copy-done.4), channel_id=1, source_target_pairs={{0,8},{8,0},{16,24},{24,16},{1,9},{9,1},{17,25},{25,17},{2,10},{10... | collective-permute-start | bytes 3080 | tf_op jit(solution)/shard_map/ppermute | solution.py:370
  12.3 6.8 %copy-start.5 = (s32[2,128]{1,0:T(2,128)}, s32[2,128]{1,0:T(2,128)S(1)}, u32[]{:S(2)}) copy-start(s32[2,128]{1,0:T(2,128)S(1)} %collective-permute-done.1.other_mask_ref) | copy-start | bytes 3076
  12.3 6.8 %copy-start.2 = (bf16[2,128,128]{2,1,0:T(8,128)(2,1)}, bf16[2,128,128]{2,1,0:T(8,128)(2,1)S(1)}, u32[]{:S(2)}) copy-start(bf16[2,128,128]{2,1,0:T(8,128)(2,1)S(1)} %collective-permute-done.other_ref) | copy-start | bytes 196612
  19.1 0.7 %copy-start = (bf16[32,24,128]{2,1,0:T(8,128)(2,1)}, bf16[32,24,128]{2,1,0:T(8,128)(2,1)S(1)}, u32[]{:S(2)}) copy-start(bf16[32,24,128]{2,1,0:T(8,128)(2,1)S(1)} %all-to-all-done.sent_ref) | copy-start | bytes 589828

commit v2 on v1

--- a/solution.py
+++ b/solution.py
@@ -182,6 +182,8 @@
 
 LANES = 128
 EXTRA = 8
+COUNTS = 3
+KERNEL_VMEM = 16 * 2**20
 
 
 def fits(queries, page_vectors, devices):
@@ -191,6 +193,7 @@
         queries.shape[0] == 1
         and tokens % 8 == 0
         and LANES % tokens == 0
+        and COUNTS + page_vectors.shape[0] <= EXTRA
         and features == LANES
         and page_vectors.shape[1] == LANES
         and lanes % LANES == 0
@@ -217,7 +220,25 @@
     return high, value - high
 
 
-def middle_kernel(tokens, sent_ref, own_ref, other_ref, own_mask_ref, other_mask_ref, out_ref, weight_ref, stat_ref):
+def first_kernel(target_ref, queries_ref, query_mask_ref, page_mask_ref, out_ref):
+    devices, _, _ = out_ref.shape
+    tokens = queries_ref.shape[1]
+    target = target_ref[0]
+    alive = jnp.sum(query_mask_ref[...].astype(jnp.float32), axis=1, keepdims=True)
+    row = lax.broadcasted_iota(jnp.int32, (EXTRA, LANES), 0)
+    extra = jnp.where(row == 0, alive, 0.0)
+    extra = jnp.where(row == 1, (target // 256).astype(jnp.float32), extra)
+    extra = jnp.where(row == 2, (target % 256).astype(jnp.float32), extra)
+    for number in range(page_mask_ref.shape[0]):
+        count = jnp.sum(page_mask_ref[number : number + 1, :].astype(jnp.float32), axis=1, keepdims=True)
+        extra = jnp.where(row == COUNTS + number, count, extra)
+    out_ref[:, 0:tokens, :] = jnp.broadcast_to(queries_ref[...], (devices, tokens, LANES))
+    out_ref[:, tokens : tokens + EXTRA, :] = jnp.broadcast_to(
+        extra.astype(jnp.bfloat16)[None], (devices, EXTRA, LANES)
+    )
+
+
+def middle_kernel(tokens, sent_ref, own_ref, other_ref, out_ref, weight_ref, stat_ref):
     sources = sent_ref.shape[0]
     lanes = sources * tokens
     chunks = lanes // LANES
@@ -226,10 +247,7 @@
     blk = lax.axis_index("blk")
     group = lax.axis_index("group")
     members = lax.axis_size("group")
-    bases = [
-        (blk * members + group) * local_pages,
-        ((blk ^ 1) * members + group) * local_pages,
-    ]
+    homes = [blk * members + group, (blk ^ 1) * members + group]
 
     extra = sent_ref[:, tokens : tokens + EXTRA, :].astype(jnp.float32)
     slot = lax.broadcasted_iota(jnp.int32, (EXTRA, LANES), 1) // tokens
@@ -240,18 +258,17 @@
             total = jnp.where(slot == i, extra[chunk * per_chunk + i], total)
         rows.append(total)
     rows = jnp.concatenate(rows, axis=1)
-    alive = rows[0:1]
+    spot = lax.broadcasted_iota(jnp.int32, (1, lanes), 1) % tokens
+    alive = (spot.astype(jnp.float32) < rows[0:1]).astype(jnp.float32)
     target = (rows[1:2] * 256.0 + rows[2:3]).astype(jnp.int32)
 
     rows_q = sent_ref[:, 0:tokens, :].reshape(lanes, LANES)
     patch = lax.broadcasted_iota(jnp.int32, (LANES, lanes), 0).astype(jnp.float32)
     tokens_soft, weights, ids = [], [], []
-    for vectors_ref, mask_ref, base in (
-        (own_ref, own_mask_ref, bases[0]),
-        (other_ref, other_mask_ref, bases[1]),
-    ):
+    for vectors_ref, home in ((own_ref, homes[0]), (other_ref, homes[1])):
+        facts = sent_ref[home, tokens : tokens + EXTRA, :].astype(jnp.float32)
         for number in range(local_pages):
-            count = jnp.sum(mask_ref[number : number + 1, :].astype(jnp.float32), axis=1, keepdims=True)
+            count = facts[COUNTS + number : COUNTS + number + 1, 0:1]
             similarity = lax.dot_general(
                 vectors_ref[number], rows_q, (((1,), (1,)), ((), ())), preferred_element_type=jnp.float32
             )
@@ -262,7 +279,7 @@
             lse = highest + jnp.log(total)
             tokens_soft.append(alive * (relaxation_scale_factor * (lse - jnp.log(count))))
             weights.append(powers * (1.0 / total))
-            ids.append(base + number)
+            ids.append(home * local_pages + number)
     scores = segment_sum(jnp.concatenate(tokens_soft, axis=0), tokens)
     top = jnp.max(scores, axis=0, keepdims=True)
     chip_lse = top + jnp.log(jnp.sum(jnp.exp(scores - top), axis=0, keepdims=True))
@@ -367,19 +384,17 @@
     blocks = lax.axis_size("blk")
     swap = [(b, b ^ 1) for b in range(blocks)]
     other_vectors = lax.ppermute(page_vectors, "blk", swap)
-    other_mask = lax.ppermute(page_mask, "blk", swap)
-
-    kind = lax.broadcasted_iota(jnp.int32, (1, EXTRA, LANES), 1)
-    number = positive[:, None, None]
-    extra = jnp.where(
-        kind == 0,
-        jnp.tile(query_mask, (1, LANES // tokens))[:, None, :],
-        jnp.where(kind == 1, number // 256, number % 256),
-    ).astype(jnp.bfloat16)
-    message = jnp.concatenate([queries, extra], axis=1)
-    sent = exchange(jnp.broadcast_to(message, (devices, tokens + EXTRA, LANES)))
 
     vmem = pl.BlockSpec(memory_space=pltpu.VMEM)
+    params = pltpu.CompilerParams(vmem_limit_bytes=KERNEL_VMEM)
+    message = pl.pallas_call(
+        first_kernel,
+        out_shape=jax.ShapeDtypeStruct((devices, tokens + EXTRA, LANES), jnp.bfloat16),
+        in_specs=[pl.BlockSpec(memory_space=pltpu.SMEM)] + [vmem] * 3,
+        out_specs=vmem,
+        compiler_params=params,
+    )(positive, queries, query_mask, page_mask)
+    sent = exchange(message)
     out, weights, stats = pl.pallas_call(
         functools.partial(middle_kernel, tokens),
         out_shape=(
@@ -387,9 +402,10 @@
             jax.ShapeDtypeStruct((local_pages, LANES, lanes), jnp.float32),
             jax.ShapeDtypeStruct((2 * local_pages, lanes), jnp.float32),
         ),
-        in_specs=[vmem] * 5,
+        in_specs=[vmem] * 3,
         out_specs=(vmem, vmem, vmem),
-    )(sent, page_vectors, other_vectors, page_mask, other_mask)
+        compiler_params=params,
+    )(sent, page_vectors, other_vectors)
     got = exchange(out.astype(jnp.float16)).astype(jnp.float32)
     grad_q, grad_p, loss = pl.pallas_call(
         functools.partial(last_kernel, tokens),
@@ -400,6 +416,7 @@
         ),
         in_specs=[vmem] * 4,
         out_specs=(vmem, vmem, vmem),
+        compiler_params=params,
     )(got, sent, weights, stats)
     return (grad_q, grad_p, loss[0, 0])
 

time: 38.6 us -> 32.4 us (0.84)
  Pallas kernels: 5.27 us -> 3.08 us
  local copies, waits for them, and re-layouts: 2.74 us -> 0.69 us
  other arithmetic: 1.88 us -> 0.06 us
    convert_element_type x2, other arithmetic: 1.79 us -> 0.06 us  [two_exchanges(): got = exchange(out.astype(jnp.float16)).astype(jnp.float32)]
    pallas_call x1, Pallas kernels: 3.06 us -> 1.37 us  [two_exchanges(): pl.pallas_call(functools.partial(middle_kernel, tokens), out_shape=(jax.S...]
    pallas_call x1, Pallas kernels: 2.21 us -> 0.95 us  [two_exchanges(): pl.pallas_call(functools.partial(last_kernel, tokens), out_shape=(jax.Sha...]
    unnamed x14 -> x8, local copies, waits for them, and re-layouts: 1.95 us -> 0.69 us
    ppermute x1, waiting for transfers between devices: 0.01 us -> 1 us  [two_exchanges(): other_vectors = lax.ppermute(page_vectors, 'blk', swap)]
    ppermute x1 -> x0, waiting for transfers between devices: 0.9 us -> none  [two_exchanges(): other_mask = lax.ppermute(page_mask, 'blk', swap)]
    broadcast_in_dim x2 -> x0, local copies, waits for them, and re-layouts: 0.79 us -> none  [the longest x1 0.71 us: two_exchanges(): sent = exchange(jnp.broadcast_to(message, (devices, tokens + EXTRA, LANES)))]
    pallas_call x0 -> x1, Pallas kernels: none -> 0.76 us  [two_exchanges(): pl.pallas_call(first_kernel, out_shape=jax.ShapeDtypeStruct((devices, tok...]
  transfers between devices with their start and end apart: 3 -> 2, of which waited for: 2 -> 2; matrix products, arithmetic and copies ran while one was open for 0% -> 0% of each run, Pallas kernels for 0% -> 0%
where the time goes in v2:
time: 32.4 us; the launch traced here: 32.2 us
  blocking collectives  11.4 us (35%)
  waiting for transfers between devices  7.94 us (25%)
  starting transfers between devices  7.64 us (24%)
  Pallas kernels  3.08 us (10%)
  between operations  1.37 us (4%)
  local copies, waits for them, and re-layouts  0.69 us (2%)
    all_to_all x1, blocking collectives, exchange(): return lax.all_to_all(blocks_to_all, ('blk', 'group'), 0, 0, tiled=True)  11.4 us
    all_to_all x1, starting transfers between devices, exchange(): return lax.all_to_all(blocks_to_all, ('blk', 'group'), 0, 0, tiled=True)  7.33 us
    all_to_all x1, waiting for transfers between devices, exchange(): return lax.all_to_all(blocks_to_all, ('blk', 'group'), 0, 0, tiled=True)  6.93 us
    pallas_call x1, Pallas kernels, two_exchanges(): pl.pallas_call(functools.partial(middle_kernel, tokens), out_shape=(jax.S...  1.37 us
    ppermute x1, waiting for transfers between devices, two_exchanges(): other_vectors = lax.ppermute(page_vectors, 'blk', swap)  1 us
    pallas_call x1, Pallas kernels, two_exchanges(): pl.pallas_call(functools.partial(last_kernel, tokens), out_shape=(jax.Sha...  0.95 us
    pallas_call x1, Pallas kernels, two_exchanges(): pl.pallas_call(first_kernel, out_shape=jax.ShapeDtypeStruct((devices, tok...  0.76 us
    unnamed x8, local copies, waits for them, and re-layouts  0.69 us
  transfers between devices with their start and end apart: 2, of which 2 were waited for; matrix products, arithmetic and copies ran while one was open for 0% of the time, Pallas kernels for 0%

profile of v2, /device:TPU:0, one launch (start us, length us, event | category | flops | bytes accessed | tf_op | source)
XLA Modules:
  0.0 32.2 jit_solution(3387796864467659244)
XLA Ops:
  0.6 0.0 copy-start.2
  0.6 0.0 copy-start.3
  1.3 0.0 copy-done.2
  1.3 0.0 copy-done.3
  1.3 0.0 copy-start.1
  1.3 0.7 %copy-done.1 = bf16[1,16,128]{2,1,0:T(8,128)(2,1)S(1)} copy-done((bf16[1,16,128]{2,1,0:T(8,128)(2,1)S(1)}, bf16[1,16,128]{2,1,0:T(8,128)(2,1)}, u32[]{:S(2)}) %copy-start.1) | copy-done | bytes 4120
  2.0 0.8 %shard_map.76 = bf16[32,24,128]{2,1,0:T(8,128)(2,1)} custom-call(s32[1]{0:T(128)S(6)} %copy.8.target_ref, bf16[1,16,128]{2,1,0:T(8,128)(2,1)S(1)} %copy-done.1, s32[1,16]{1,0:T(1,128)S(1)} %copy-done.3, s32[2,128]{1,0:T(2,128)S(1)} %copy-done.2), custom_call_target="tpu_custom_call" | custom-call | tf_op jit(solution)/shard_map/pallas_call | solution.py:390
  2.8 0.0 copy-start
  2.8 7.3 %all-to-all-start = ((bf16[32,24,128]{2,1,0:T(8,128)(2,1)}), bf16[32,24,128]{2,1,0:T(8,128)(2,1)S(1)}, u32[]{:S(2)}, u32[]{:S(2)}) async-start(bf16[32,24,128]{2,1,0:T(8,128)(2,1)} %shard_map.76), calls=%async_computation | async-start | bytes 393216 | tf_op jit(solution)/shard_map/all_to_all | solution.py:376
  10.1 0.0 copy-done
  10.1 0.3 collective-permute-start
  10.4 1.0 %collective-permute-done.other_ref = bf16[2,128,128]{2,1,0:T(8,128)(2,1)S(1)} collective-permute-done((bf16[2,128,128]{2,1,0:T(8,128)(2,1)S(1)}, bf16[2,128,128]{2,1,0:T(8,128)(2,1)S(1)}, u32[]{:S(2)}, u32[]{:S(2)}) %collective-permute-start) | collective-permute-done | bytes 65568 | tf_op jit(solution)/shard_map/ppermute | solution.py:386
  11.4 6.9 %all-to-all-done.sent_ref = bf16[32,24,128]{2,1,0:T(8,128)(2,1)S(1)} async-done(((bf16[32,24,128]{2,1,0:T(8,128)(2,1)}), bf16[32,24,128]{2,1,0:T(8,128)(2,1)S(1)}, u32[]{:S(2)}, u32[]{:S(2)}) %all-to-all-start) | async-done | bytes 196640 | tf_op jit(solution)/shard_map/all_to_all | solution.py:376
  18.4 1.4 %shard_map.77 = (f32[32,24,128]{2,1,0:T(8,128)S(1)}, f32[2,128,512]{2,1,0:T(8,128)S(1)}, f32[4,512]{1,0:T(4,128)S(1)}) custom-call(bf16[32,24,128]{2,1,0:T(8,128)(2,1)S(1)} %all-to-all-done.sent_ref, bf16[2,128,128]{2,1,0:T(8,128)(2,1)S(1)} %copy-done, bf16[2,128,128]{2,1,0:T(8,128)(2,1)S(1)} %collective-permute-done.other_ref), custom_call_target="tpu_custom_call" | custom-call | tf_op jit(solution)/shard_map/pallas_call | solution.py:398
  19.8 11.4 %all_to_all.10 = f16[32,24,128]{2,1,0:T(8,128)(2,1)S(1)} all-to-all(f16[32,24,128]{2,1,0:T(8,128)(2,1)S(1)} %convert_element_type.6), channel_id=1, replica_groups=mesh['blk'=4,'group'=8] {'blk','group'}, dimensions={0} | all-to-all | bytes 393216 | tf_op jit(solution)/shard_map/all_to_all | solution.py:376
  31.2 0.9 %shard_map.78 = (f32[1,16,128]{2,1,0:T(8,128)}, f32[2,128,128]{2,1,0:T(8,128)}, f32[1,1]{1,0:T(1,128)}) custom-call(f32[32,24,128]{2,1,0:T(8,128)S(1)} %convert_element_type.7.got_ref, bf16[32,24,128]{2,1,0:T(8,128)(2,1)S(1)} %all-to-all-done.sent_ref, f32[2,128,512]{2,1,0:T(8,128)S(1)} %get-tuple-element.10.weight_ref, f32[4,512]{1,0:T(4,128)S(1)} %get-tuple-element.11.stat_ref), custom_call_target="tpu_custom_call" | custom-call | tf_op jit(solution)/shard_map/pallas_call | solution.py:410
  (2 shorter events, 0.1 us)
Async XLA Ops:
  0.6 0.7 %copy-start.2 = (s32[2,128]{1,0:T(2,128)S(1)}, s32[2,128]{1,0:T(2,128)}, u32[]{:S(2)}) copy-start(s32[2,128]{1,0:T(2,128)} %page_mask_ref.1) | copy-start | bytes 3076
  0.6 0.7 %copy-start.3 = (s32[1,16]{1,0:T(1,128)S(1)}, s32[1,16]{1,0:T(1,128)}, u32[]{:S(2)}) copy-start(s32[1,16]{1,0:T(1,128)} %query_mask_ref.1) | copy-start | bytes 196
  1.3 0.7 %copy-start.1 = (bf16[1,16,128]{2,1,0:T(8,128)(2,1)S(1)}, bf16[1,16,128]{2,1,0:T(8,128)(2,1)}, u32[]{:S(2)}) copy-start(bf16[1,16,128]{2,1,0:T(8,128)(2,1)} %queries_ref.1) | copy-start | bytes 12292
  2.8 7.3 %copy-start = (bf16[2,128,128]{2,1,0:T(8,128)(2,1)S(1)}, bf16[2,128,128]{2,1,0:T(8,128)(2,1)}, u32[]{:S(2)}) copy-start(bf16[2,128,128]{2,1,0:T(8,128)(2,1)} %own_ref.1) | copy-start | bytes 196612
  2.8 15.6 %all-to-all-start = ((bf16[32,24,128]{2,1,0:T(8,128)(2,1)}), bf16[32,24,128]{2,1,0:T(8,128)(2,1)S(1)}, u32[]{:S(2)}, u32[]{:S(2)}) async-start(bf16[32,24,128]{2,1,0:T(8,128)(2,1)} %shard_map.76), calls=%async_computation | async-start | bytes 393216 | tf_op jit(solution)/shard_map/all_to_all | solution.py:376
  10.1 1.3 %collective-permute-start = (bf16[2,128,128]{2,1,0:T(8,128)(2,1)S(1)}, bf16[2,128,128]{2,1,0:T(8,128)(2,1)S(1)}, u32[]{:S(2)}, u32[]{:S(2)}) collective-permute-start(bf16[2,128,128]{2,1,0:T(8,128)(2,1)S(1)} %copy-done), channel_id=1, source_target_pairs={{0,8},{8,0},{16,24},{24,16},{1,9},{9,1},{17,25},{25,17},{2,10},{10... | collective-permute-start | bytes 196616 | tf_op jit(solution)/shard_map/ppermute | solution.py:386

commit v3 on v0

--- a/solution.py
+++ b/solution.py
@@ -1,8 +1,11 @@
+import functools
 import math
 
 import jax
 import jax.numpy as jnp
 from jax import lax
+from jax.experimental import pallas as pl
+from jax.experimental.pallas import tpu as pltpu
 from jax.sharding import PartitionSpec as P
 
 relaxation_scale_factor = 0.5
@@ -43,7 +46,7 @@
     return (highest, totals, earlier[2] + later[2])
 
 
-def on_device(queries, query_mask, positive, page_vectors, page_mask):
+def general_path(queries, query_mask, positive, page_vectors, page_mask):
     tokens = queries.shape[1]
     features = queries.shape[2]
     local_pages = page_vectors.shape[0]
@@ -177,6 +180,325 @@
     return (grad_queries, page_grads, mean_loss)
 
 
+LANES = 128
+EXTRA = 2
+FACTS = 16
+WIDE_FIRST = 256
+WIDE_SECOND = 256
+KERNEL_VMEM = 16 * 2**20
+
+
+def fits(queries, page_vectors, devices):
+    tokens, features = queries.shape[1:]
+    lanes = devices * tokens
+    return (
+        queries.shape[0] == 1
+        and tokens == FACTS
+        and features == LANES
+        and page_vectors.shape[1] == LANES
+        and page_vectors.shape[0] <= FACTS - 3
+        and lanes % LANES == 0
+        and lanes // LANES <= 8
+        and lax.axis_size("blk") % 2 == 0
+    )
+
+
+def segment_sum(values, width):
+    lanes = values.shape[1]
+    lane = lax.broadcasted_iota(jnp.int32, values.shape, 1)
+    step = 1
+    while step < width:
+        ahead = pltpu.roll(values, lanes - step, 1)
+        behind = pltpu.roll(values, step, 1)
+        values = values + jnp.where((lane & step) == 0, ahead, behind)
+        step *= 2
+    return values
+
+
+def spread_runs(line, width):
+    lane = lax.broadcasted_iota(jnp.int32, (8, LANES), 1)
+    row = lax.broadcasted_iota(jnp.int32, (8, LANES), 0)
+    return jnp.take_along_axis(jnp.broadcast_to(line, (8, LANES)), lane // width * width + row, axis=1)
+
+
+def split_half(value):
+    scaled = value * 8193.0
+    high = scaled - (scaled - value)
+    return high, value - high
+
+
+def first_kernel(target_ref, queries_ref, query_mask_ref, page_mask_ref, out_ref, *scratch):
+    target, queries, query_mask, page_mask, message, sems, out_sem = scratch
+    devices = out_ref.shape[0]
+    tokens = queries_ref.shape[1]
+    loads = [
+        pltpu.make_async_copy(src, dst, sems.at[i])
+        for i, (src, dst) in enumerate(
+            (
+                (queries_ref, queries),
+                (query_mask_ref, query_mask),
+                (page_mask_ref, page_mask),
+                (target_ref, target),
+            )
+        )
+    ]
+    for load in loads:
+        load.start()
+    for load in loads:
+        load.wait()
+    alive = jnp.sum(query_mask[...].astype(jnp.float32), axis=1, keepdims=True)
+    kind = lax.broadcasted_iota(jnp.int32, (EXTRA, LANES), 1) % FACTS
+    number = target[0]
+    facts = jnp.where(kind == 0, alive, 0.0)
+    facts = jnp.where(kind == 1, (number >> 8).astype(jnp.float32), facts)
+    facts = jnp.where(kind == 2, (number & 255).astype(jnp.float32), facts)
+    for page in range(page_mask.shape[0]):
+        count = jnp.sum(page_mask[page : page + 1, :].astype(jnp.float32), axis=1, keepdims=True)
+        facts = jnp.where(kind == 3 + page, count, facts)
+    for pair in range(tokens // 2):
+        message[:, pair] = jnp.broadcast_to(queries[:, 2 * pair : 2 * pair + 2, :], (devices, 2, LANES))
+    message[:, tokens // 2] = jnp.broadcast_to(facts.astype(jnp.bfloat16)[None], (devices, EXTRA, LANES))
+    store = pltpu.make_async_copy(message, out_ref, out_sem)
+    store.start()
+    store.wait()
+
+
+def middle_kernel(tokens, sent_ref, own_ref, other_ref, out_ref, power_ref, stat_ref, rows_ref, other_power_ref):
+    sources = sent_ref.shape[0]
+    lanes = sources * tokens
+    chunks = lanes // LANES
+    per_chunk = LANES // tokens
+    local_pages = own_ref.shape[0]
+    blk = lax.axis_index("blk")
+    group = lax.axis_index("group")
+    members = lax.axis_size("group")
+    homes = [blk * members + group, (blk ^ 1) * members + group]
+    sends_sum = (blk & 1) == 0
+
+    counts, ids, vectors, powers_refs = [], [], [], []
+    for vectors_ref, kept_ref, home in ((own_ref, power_ref, homes[0]), (other_ref, other_power_ref, homes[1])):
+        facts = sent_ref[home, tokens // 2].astype(jnp.float32)
+        for number in range(local_pages):
+            counts.append(facts[0:1, 3 + number : 4 + number])
+            ids.append(home * local_pages + number)
+            vectors.append(vectors_ref[number])
+            powers_refs.append(kept_ref.at[number])
+    slot = lax.broadcasted_iota(jnp.int32, (1, LANES), 1) // tokens
+    spot = lax.broadcasted_iota(jnp.int32, (1, LANES), 1) % tokens
+    steep = 1.0 / (relaxation_scale_factor * math.log(2.0))
+
+    scales = []
+    high_line = jnp.zeros((1, LANES), jnp.float32)
+    low_line = jnp.zeros((1, LANES), jnp.float32)
+    wide_first = math.gcd(WIDE_FIRST, lanes)
+    for start in range(0, lanes, wide_first):
+        columns = pl.ds(start, wide_first)
+        facts = []
+        for c in range(start // LANES, (start + wide_first) // LANES):
+            told = jnp.zeros((1, LANES), jnp.float32)
+            for i in range(per_chunk):
+                told = jnp.where(
+                    slot == i, sent_ref[c * per_chunk + i, tokens // 2, 0:1, :].astype(jnp.float32), told
+                )
+            facts.append(spread_runs(told, tokens))
+        facts = jnp.concatenate(facts, axis=1)
+        spots = lax.broadcasted_iota(jnp.int32, (1, wide_first), 1) % tokens
+        alive = (spots.astype(jnp.float32) < facts[0:1]).astype(jnp.float32)
+        target = (facts[1:2] * 256.0 + facts[2:3]).astype(jnp.int32)
+        first, last = start // tokens, (start + wide_first) // tokens
+        rows_q = sent_ref[first:last, 0 : tokens // 2].reshape(wide_first, LANES)
+        rows_ref[columns, :] = rows_q
+
+        softened, inverses = [], []
+        patch = lax.broadcasted_iota(jnp.int32, (LANES, wide_first), 0).astype(jnp.float32)
+        for page in range(2 * local_pages):
+            similarity = lax.dot_general(
+                vectors[page], rows_q, (((1,), (1,)), ((), ())), preferred_element_type=jnp.float32
+            )
+            masked = jnp.where(patch < counts[page], similarity, guarded_floor_entry)
+            highest = jnp.max(masked, axis=0, keepdims=True)
+            powers = jnp.exp2((masked - highest) * steep)
+            powers_refs[page][:, columns] = powers
+            total = jnp.sum(powers, axis=0, keepdims=True)
+            lse = highest * (1.0 / relaxation_scale_factor) + jnp.log(total)
+            softened.append(alive * (relaxation_scale_factor * (lse - jnp.log(counts[page]))))
+            inverses.append(alive / total)
+        scores = segment_sum(jnp.concatenate(softened, axis=0), tokens)
+        top = jnp.max(scores, axis=0, keepdims=True)
+        chip_lse = top + jnp.log(jnp.sum(jnp.exp(scores - top), axis=0, keepdims=True))
+
+        picked = jnp.zeros((1, wide_first), jnp.float32)
+        chunk_scales = []
+        for page in range(2 * local_pages):
+            score = scores[page : page + 1]
+            hit = target == ids[page]
+            picked = picked + jnp.where(hit, score, 0.0)
+            share = jnp.where(sends_sum, jnp.exp(score - chip_lse), hit.astype(jnp.float32))
+            chunk_scales.append(inverses[page] * share)
+            if page < local_pages:
+                for row, value in enumerate((score, hit.astype(jnp.float32), inverses[page])):
+                    stat_ref[row * local_pages + page : row * local_pages + page + 1, columns] = value
+        scales.append(chunk_scales)
+        high, low = split_half(jnp.where(sends_sum, chip_lse, picked))
+        for offset in range(0, wide_first, LANES):
+            c = (start + offset) // LANES
+            high_line = jnp.where(spot == c, high[:, offset : offset + LANES], high_line)
+            low_line = jnp.where(spot == c, low[:, offset : offset + LANES], low_line)
+
+    scales = [jnp.concatenate([part[page] for part in scales], axis=1) for page in range(2 * local_pages)]
+    flipped = jnp.concatenate(vectors, axis=0).T
+    wide_second = math.gcd(WIDE_SECOND, lanes)
+    for start in range(0, lanes, wide_second):
+        highs, lows = [], []
+        for page in range(2 * local_pages):
+            term = powers_refs[page][:, pl.ds(start, wide_second)] * scales[page][:, start : start + wide_second]
+            high = term.astype(jnp.bfloat16)
+            highs.append(high)
+            lows.append((term - high.astype(jnp.float32)).astype(jnp.bfloat16))
+        mixed = jnp.dot(flipped, jnp.concatenate(highs, axis=0), preferred_element_type=jnp.float32) + jnp.dot(
+            flipped, jnp.concatenate(lows, axis=0), preferred_element_type=jnp.float32
+        )
+        first, last = start // tokens, (start + wide_second) // tokens
+        out_ref[first:last, 0 : tokens // 2] = mixed.T.reshape(last - first, tokens // 2, 2, LANES)
+    lines = jnp.concatenate([high_line, low_line], axis=0)
+    out_ref[:, tokens // 2] = jnp.broadcast_to(lines[None], (sources, EXTRA, LANES))
+
+
+def last_kernel(tokens, got_ref, rows_ref, power_ref, stat_ref, grad_q_out, grad_p_out, loss_out, *scratch):
+    grad_q_ref, grad_p_ref, loss_ref, sems = scratch
+    sources = got_ref.shape[0]
+    lanes = sources * tokens
+    chunks = lanes // LANES
+    per_chunk = LANES // tokens
+    local_pages = power_ref.shape[0]
+    blk = lax.axis_index("blk")
+    group = lax.axis_index("group")
+    members = lax.axis_size("group")
+    me = blk * members + group
+    even = [s for s in range(sources) if (s // members) % 2 == 0]
+    odd = [s for s in range(sources) if (s // members) % 2 == 1]
+
+    def stats(source):
+        return got_ref[source, tokens // 2, 0:1, :] + got_ref[source, tokens // 2, 1:2, :]
+
+    def tree(combine, values):
+        while len(values) > 1:
+            values = [combine(*values[i : i + 2]) if i + 1 < len(values) else values[i] for i in range(0, len(values), 2)]
+        return values[0]
+
+    chip_lse = [stats(s) for s in even]
+    top = tree(jnp.maximum, chip_lse)
+    page_lse = top + jnp.log(tree(jnp.add, [jnp.exp(c - top) for c in chip_lse]))
+    spread = spread_runs(page_lse, tokens)
+    flat = jnp.concatenate([spread[c : c + 1] for c in range(chunks)], axis=1)
+    rows_q = rows_ref[...]
+    copies = []
+    for page in range(local_pages):
+        score, hit, inverse = (
+            stat_ref[row * local_pages + page : row * local_pages + page + 1, :] for row in range(3)
+        )
+        coefficient = (jnp.exp(score - flat) - hit) * inverse
+        factor = (coefficient * power_ref[page]).astype(jnp.bfloat16)
+        grad_p_ref[page] = jnp.dot(factor, rows_q, preferred_element_type=jnp.float32)
+        copies.append(pltpu.make_async_copy(grad_p_ref.at[page], grad_p_out.at[page], sems.at[page]))
+        copies[-1].start()
+
+    lane = lax.broadcasted_iota(jnp.int32, (1, LANES), 1)
+    mine = lane == (me % per_chunk) * tokens + me // per_chunk
+    ratios = jnp.concatenate([jnp.where(mine, jnp.exp(c - page_lse), 0.0) for c in chip_lse], axis=0)
+    ratios = jnp.broadcast_to(jnp.sum(ratios, axis=1, keepdims=True), ratios.shape)
+    grad_q = jnp.zeros((tokens // 2, 2, LANES), jnp.float32)
+    for i, s in enumerate(even):
+        grad_q = grad_q + ratios[i : i + 1, :][None] * got_ref[s, 0 : tokens // 2]
+    for s in odd:
+        grad_q = grad_q - got_ref[s, 0 : tokens // 2]
+    for pair in range(tokens // 2):
+        grad_q_ref[0, 2 * pair : 2 * pair + 2, :] = grad_q[pair]
+    copies.append(pltpu.make_async_copy(grad_q_ref, grad_q_out, sems.at[local_pages]))
+    copies[-1].start()
+
+    picked = tree(jnp.add, [stats(s) for s in odd])
+    difference = jnp.where(lane % tokens < chunks, page_lse - picked, 0.0)
+    loss_ref[...] = jnp.sum(difference, axis=1, keepdims=True) * (1.0 / sources)
+    copies.append(pltpu.make_async_copy(loss_ref, loss_out, sems.at[local_pages + 1]))
+    copies[-1].start()
+    for copy in copies:
+        copy.wait()
+
+
+def exchange(blocks_to_all):
+    return lax.all_to_all(blocks_to_all, ("blk", "group"), 0, 0, tiled=True)
+
+
+def two_exchanges(queries, query_mask, positive, page_vectors, page_mask):
+    tokens = queries.shape[1]
+    local_pages = page_vectors.shape[0]
+    devices = lax.axis_size("blk") * lax.axis_size("group")
+    lanes = devices * tokens
+    blocks = lax.axis_size("blk")
+    pairs = (tokens + EXTRA) // 2
+    swap = [(b, b ^ 1) for b in range(blocks)]
+    other_vectors = lax.ppermute(page_vectors, "blk", swap)
+
+    vmem = pl.BlockSpec(memory_space=pltpu.VMEM)
+    anywhere = pl.BlockSpec(memory_space=pl.ANY)
+    params = pltpu.CompilerParams(vmem_limit_bytes=KERNEL_VMEM)
+    message = pl.pallas_call(
+        first_kernel,
+        out_shape=jax.ShapeDtypeStruct((devices, pairs, 2, LANES), jnp.bfloat16),
+        in_specs=[anywhere] * 4,
+        out_specs=anywhere,
+        scratch_shapes=[
+            pltpu.SMEM(positive.shape, jnp.int32),
+            pltpu.VMEM(queries.shape, jnp.bfloat16),
+            pltpu.VMEM(query_mask.shape, jnp.int32),
+            pltpu.VMEM(page_mask.shape, jnp.int32),
+            pltpu.VMEM((devices, pairs, 2, LANES), jnp.bfloat16),
+            pltpu.SemaphoreType.DMA((4,)),
+            pltpu.SemaphoreType.DMA,
+        ],
+    )(positive, queries, query_mask, page_mask)
+    sent = exchange(message)
+    out, powers, stats, rows_q = pl.pallas_call(
+        functools.partial(middle_kernel, tokens),
+        out_shape=(
+            jax.ShapeDtypeStruct((devices, pairs, 2, LANES), jnp.float32),
+            jax.ShapeDtypeStruct((local_pages, LANES, lanes), jnp.float32),
+            jax.ShapeDtypeStruct((3 * local_pages, lanes), jnp.float32),
+            jax.ShapeDtypeStruct((lanes, LANES), jnp.bfloat16),
+        ),
+        in_specs=[vmem] * 3,
+        out_specs=(vmem,) * 4,
+        scratch_shapes=[pltpu.VMEM((local_pages, LANES, lanes), jnp.float32)],
+        compiler_params=params,
+    )(sent, page_vectors, other_vectors)
+    got = exchange(out.astype(jnp.float16)).astype(jnp.float32)
+    grad_q, grad_p, loss = pl.pallas_call(
+        functools.partial(last_kernel, tokens),
+        out_shape=(
+            jax.ShapeDtypeStruct(queries.shape, jnp.float32),
+            jax.ShapeDtypeStruct(page_vectors.shape, jnp.float32),
+            jax.ShapeDtypeStruct((1, 1), jnp.float32),
+        ),
+        in_specs=[vmem] * 4,
+        out_specs=(anywhere,) * 3,
+        scratch_shapes=[
+            pltpu.VMEM(queries.shape, jnp.float32),
+            pltpu.VMEM(page_vectors.shape, jnp.float32),
+            pltpu.VMEM((1, 1), jnp.float32),
+            pltpu.SemaphoreType.DMA((local_pages + 2,)),
+        ],
+        compiler_params=params,
+    )(got, rows_q, powers, stats)
+    return (grad_q, grad_p, loss[0, 0])
+
+
+def on_device(queries, query_mask, positive, page_vectors, page_mask):
+    devices = lax.axis_size("blk") * lax.axis_size("group")
+    chosen = two_exchanges if fits(queries, page_vectors, devices) else general_path
+    return chosen(queries, query_mask, positive, page_vectors, page_mask)
+
+
 def solution(mesh):
     in_specs = (
         P(("blk", "group"), None, None),

time: 264 us -> 31.1 us (0.12)
  blocking collectives: 116 us -> 10.3 us
  waiting for transfers between devices: 68.8 us -> 7.57 us
  local copies, waits for them, and re-layouts: 24.5 us -> 0.01 us
  loops' own time: 21.1 us -> 0 us
  between operations: 17.3 us -> 1.33 us
  matrix products: 4.3 us -> 0 us
  Pallas kernels: 0 us -> 3.78 us
  other arithmetic: 3.58 us -> 0.21 us
    all_gather x4 -> x0, blocking collectives: 63.6 us -> none  [the longest x1 32.4 us: on_device(): lax.all_gather(queries, 'group', axis=0, tiled=True)]
    reduce_scatter x1 -> x0, waiting for transfers between devices: 63.1 us -> none  [on_device(): lax.psum_scatter(collected, 'group', scatter_dimension=0, tiled=True)]
    unnamed x3 -> x0, blocking collectives: 52.2 us -> none
    another operation x2 -> x0, loops' own time: 21.1 us -> none  [the longest x1 20.9 us: combined_all(): lax.fori_loop(1, lax.axis_size(axis), lambda source, state: combine(state...]
    dynamic_slice x37 -> x0, local copies, waits for them, and re-layouts: 18.2 us -> none  [the longest x33 18.2 us: take(): lax.dynamic_index_in_dim(a, source, 0, False)]
    all_to_all x0 -> x1, blocking collectives: none -> 10.3 us  [exchange(): return lax.all_to_all(blocks_to_all, ('blk', 'group'), 0, 0, tiled=True)]
    all_to_all x0 -> x1, starting transfers between devices: none -> 7.33 us  [exchange(): return lax.all_to_all(blocks_to_all, ('blk', 'group'), 0, 0, tiled=True)]
    ppermute x7 -> x1, starting transfers between devices: 7.4 us -> 0.32 us  [two_exchanges(): other_vectors = lax.ppermute(page_vectors, 'blk', swap)]
  transfers between devices with their start and end apart: 8 -> 2, of which waited for: 5 -> 2; matrix products, arithmetic and copies ran while one was open for 1% -> 0% of each run, Pallas kernels for 0% -> 0%
where the time goes in v3:
time: 31.1 us; the launch traced here: 30.9 us
  blocking collectives  10.3 us (33%)
  starting transfers between devices  7.65 us (25%)
  waiting for transfers between devices  7.57 us (24%)
  Pallas kernels  3.78 us (12%)
  between operations  1.33 us (4%)
    all_to_all x1, blocking collectives, exchange(): return lax.all_to_all(blocks_to_all, ('blk', 'group'), 0, 0, tiled=True)  10.3 us
    all_to_all x1, starting transfers between devices, exchange(): return lax.all_to_all(blocks_to_all, ('blk', 'group'), 0, 0, tiled=True)  7.33 us
    all_to_all x1, waiting for transfers between devices, exchange(): return lax.all_to_all(blocks_to_all, ('blk', 'group'), 0, 0, tiled=True)  6.56 us
    pallas_call x1, Pallas kernels, two_exchanges(): pl.pallas_call(first_kernel, out_shape=jax.ShapeDtypeStruct((devices, pai...  1.5 us
    pallas_call x1, Pallas kernels, two_exchanges(): pl.pallas_call(functools.partial(middle_kernel, tokens), out_shape=(jax.S...  1.27 us
    pallas_call x1, Pallas kernels, two_exchanges(): pl.pallas_call(functools.partial(last_kernel, tokens), out_shape=(jax.Sha...  1.01 us
    ppermute x1, waiting for transfers between devices, two_exchanges(): other_vectors = lax.ppermute(page_vectors, 'blk', swap)  1 us
  transfers between devices with their start and end apart: 2, of which 2 were waited for; matrix products, arithmetic and copies ran while one was open for 0% of the time, Pallas kernels for 0%

profile of v3, /device:TPU:0, one launch (start us, length us, event | category | flops | bytes accessed | tf_op | source)
XLA Modules:
  0.0 30.9 jit_solution(11153463017633612329)
XLA Ops:
  1.3 1.5 %shard_map.76 = bf16[32,9,2,128]{3,2,1,0:T(2,128)(2,1)} custom-call(s32[1]{0:T(128)S(6)} %copy.8.target_ref, bf16[1,16,128]{2,1,0:T(8,128)(2,1)} %queries_ref.1, s32[1,16]{1,0:T(1,128)} %query_mask_ref.1, s32[2,128]{1,0:T(2,128)} %page_mask_ref.1), custom_call_target="tpu_custom_call" | custom-call | tf_op jit(solution)/shard_map/pallas_call | solution.py:446
  2.8 0.0 copy-start
  2.8 7.3 %all-to-all-start = ((bf16[32,9,2,128]{3,2,1,0:T(2,128)(2,1)}), bf16[32,9,2,128]{3,2,1,0:T(2,128)(2,1)S(1)}, u32[]{:S(2)}, u32[]{:S(2)}) async-start(bf16[32,9,2,128]{3,2,1,0:T(2,128)(2,1)} %shard_map.76), calls=%async_computation | async-start | bytes 294912 | tf_op jit(solution)/shard_map/all_to_all | solution.py:430
  10.1 0.0 copy-done
  10.1 0.3 %collective-permute-start = (bf16[2,128,128]{2,1,0:T(8,128)(2,1)S(1)}, bf16[2,128,128]{2,1,0:T(8,128)(2,1)S(1)}, u32[]{:S(2)}, u32[]{:S(2)}) collective-permute-start(bf16[2,128,128]{2,1,0:T(8,128)(2,1)S(1)} %copy-done), channel_id=1, source_target_pairs={{0,8},{8,0},{16,24},{24,16},{1,9},{9,1},{17,25},{25,17},{2,10},{10... | collective-permute-start | bytes 196616 | tf_op jit(solution)/shard_map/ppermute | solution.py:441
  10.5 1.0 %collective-permute-done.other_ref = bf16[2,128,128]{2,1,0:T(8,128)(2,1)S(1)} collective-permute-done((bf16[2,128,128]{2,1,0:T(8,128)(2,1)S(1)}, bf16[2,128,128]{2,1,0:T(8,128)(2,1)S(1)}, u32[]{:S(2)}, u32[]{:S(2)}) %collective-permute-start) | collective-permute-done | bytes 65568 | tf_op jit(solution)/shard_map/ppermute | solution.py:441
  11.5 6.6 %all-to-all-done.sent_ref = bf16[32,9,2,128]{3,2,1,0:T(2,128)(2,1)S(1)} async-done(((bf16[32,9,2,128]{3,2,1,0:T(2,128)(2,1)}), bf16[32,9,2,128]{3,2,1,0:T(2,128)(2,1)S(1)}, u32[]{:S(2)}, u32[]{:S(2)}) %all-to-all-start) | async-done | bytes 147488 | tf_op jit(solution)/shard_map/all_to_all | solution.py:430
  18.0 1.3 %shard_map.77 = (f32[32,9,2,128]{3,2,1,0:T(2,128)S(1)}, f32[2,128,512]{2,1,0:T(8,128)S(1)}, f32[6,512]{1,0:T(8,128)S(1)}, bf16[512,128]{1,0:T(8,128)(2,1)S(1)}) custom-call(bf16[32,9,2,128]{3,2,1,0:T(2,128)(2,1)S(1)} %all-to-all-done.sent_ref, bf16[2,128,128]{2,1,0:T(8,128)(2,1)S(1)} %copy-done, bf16[2,128,128]{2,1,0:T(8,128)(2,1)S(1)} %collective-permute-done.other_ref), custom_call_target="tpu_custom_call" | custom-call | tf_op jit(solution)/shard_map/pallas_call | solution.py:462
  19.3 0.1 convert_element_type.6
  19.4 10.3 %all_to_all.10 = f16[32,9,2,128]{3,2,1,0:T(2,128)(2,1)S(1)} all-to-all(f16[32,9,2,128]{3,2,1,0:T(2,128)(2,1)S(1)} %convert_element_type.6), channel_id=1, replica_groups=mesh['blk'=4,'group'=8] {'blk','group'}, dimensions={0} | all-to-all | bytes 294912 | tf_op jit(solution)/shard_map/all_to_all | solution.py:430
  29.7 0.1 convert_element_type.7.got_ref
  29.9 1.0 %shard_map.78 = (f32[1,16,128]{2,1,0:T(8,128)}, f32[2,128,128]{2,1,0:T(8,128)}, f32[1,1]{1,0:T(1,128)}) custom-call(f32[32,9,2,128]{3,2,1,0:T(2,128)S(1)} %convert_element_type.7.got_ref, bf16[512,128]{1,0:T(8,128)(2,1)S(1)} %get-tuple-element.11.rows_ref, f32[2,128,512]{2,1,0:T(8,128)S(1)} %get-tuple-element.12.power_ref, ...), custom_call_target="tpu_custom_call" | custom-call | tf_op jit(solution)/shard_map/pallas_call | solution.py:476
Async XLA Ops:
  2.8 7.4 %copy-start = (bf16[2,128,128]{2,1,0:T(8,128)(2,1)S(1)}, bf16[2,128,128]{2,1,0:T(8,128)(2,1)}, u32[]{:S(2)}) copy-start(bf16[2,128,128]{2,1,0:T(8,128)(2,1)} %own_ref.1) | copy-start | bytes 196612
  2.8 15.2 %all-to-all-start = ((bf16[32,9,2,128]{3,2,1,0:T(2,128)(2,1)}), bf16[32,9,2,128]{3,2,1,0:T(2,128)(2,1)S(1)}, u32[]{:S(2)}, u32[]{:S(2)}) async-start(bf16[32,9,2,128]{3,2,1,0:T(2,128)(2,1)} %shard_map.76), calls=%async_computation | async-start | bytes 294912 | tf_op jit(solution)/shard_map/all_to_all | solution.py:430
  10.1 1.3 %collective-permute-start = (bf16[2,128,128]{2,1,0:T(8,128)(2,1)S(1)}, bf16[2,128,128]{2,1,0:T(8,128)(2,1)S(1)}, u32[]{:S(2)}, u32[]{:S(2)}) collective-permute-start(bf16[2,128,128]{2,1,0:T(8,128)(2,1)S(1)} %copy-done), channel_id=1, source_target_pairs={{0,8},{8,0},{16,24},{24,16},{1,9},{9,1},{17,25},{25,17},{2,10},{10... | collective-permute-start | bytes 196616 | tf_op jit(solution)/shard_map/ppermute | solution.py:441

commit v4 on v3

--- a/solution.py
+++ b/solution.py
@@ -228,7 +228,7 @@
 
 
 def first_kernel(target_ref, queries_ref, query_mask_ref, page_mask_ref, out_ref, *scratch):
-    target, queries, query_mask, page_mask, message, sems, out_sem = scratch
+    queries, query_mask, page_mask, sems = scratch
     devices = out_ref.shape[0]
     tokens = queries_ref.shape[1]
     loads = [
@@ -238,7 +238,6 @@
                 (queries_ref, queries),
                 (query_mask_ref, query_mask),
                 (page_mask_ref, page_mask),
-                (target_ref, target),
             )
         )
     ]
@@ -248,19 +247,17 @@
         load.wait()
     alive = jnp.sum(query_mask[...].astype(jnp.float32), axis=1, keepdims=True)
     kind = lax.broadcasted_iota(jnp.int32, (EXTRA, LANES), 1) % FACTS
-    number = target[0]
+    number = target_ref[...].reshape(1, 1)
     facts = jnp.where(kind == 0, alive, 0.0)
     facts = jnp.where(kind == 1, (number >> 8).astype(jnp.float32), facts)
     facts = jnp.where(kind == 2, (number & 255).astype(jnp.float32), facts)
     for page in range(page_mask.shape[0]):
         count = jnp.sum(page_mask[page : page + 1, :].astype(jnp.float32), axis=1, keepdims=True)
         facts = jnp.where(kind == 3 + page, count, facts)
-    for pair in range(tokens // 2):
-        message[:, pair] = jnp.broadcast_to(queries[:, 2 * pair : 2 * pair + 2, :], (devices, 2, LANES))
-    message[:, tokens // 2] = jnp.broadcast_to(facts.astype(jnp.bfloat16)[None], (devices, EXTRA, LANES))
-    store = pltpu.make_async_copy(message, out_ref, out_sem)
-    store.start()
-    store.wait()
+    out_rows = out_ref.reshape(devices, tokens + EXTRA, LANES)
+    for device in range(devices):
+        out_rows[device, 0:tokens, :] = queries[0]
+    out_ref[:, tokens // 2] = jnp.broadcast_to(facts.astype(jnp.bfloat16)[None], (devices, EXTRA, LANES))
 
 
 def middle_kernel(tokens, sent_ref, own_ref, other_ref, out_ref, power_ref, stat_ref, rows_ref, other_power_ref):
@@ -285,6 +282,8 @@
             powers_refs.append(kept_ref.at[number])
     slot = lax.broadcasted_iota(jnp.int32, (1, LANES), 1) // tokens
     spot = lax.broadcasted_iota(jnp.int32, (1, LANES), 1) % tokens
+    sent_rows = sent_ref.reshape(sources, tokens + EXTRA, LANES)
+    out_rows = out_ref.reshape(sources, tokens + EXTRA, LANES)
     steep = 1.0 / (relaxation_scale_factor * math.log(2.0))
 
     scales = []
@@ -306,8 +305,9 @@
         alive = (spots.astype(jnp.float32) < facts[0:1]).astype(jnp.float32)
         target = (facts[1:2] * 256.0 + facts[2:3]).astype(jnp.int32)
         first, last = start // tokens, (start + wide_first) // tokens
-        rows_q = sent_ref[first:last, 0 : tokens // 2].reshape(wide_first, LANES)
-        rows_ref[columns, :] = rows_q
+        for source in range(first, last):
+            rows_ref[source * tokens : (source + 1) * tokens, :] = sent_rows[source, 0:tokens, :]
+        rows_q = rows_ref[columns, :]
 
         softened, inverses = [], []
         patch = lax.broadcasted_iota(jnp.int32, (LANES, wide_first), 0).astype(jnp.float32)
@@ -358,8 +358,9 @@
         mixed = jnp.dot(flipped, jnp.concatenate(highs, axis=0), preferred_element_type=jnp.float32) + jnp.dot(
             flipped, jnp.concatenate(lows, axis=0), preferred_element_type=jnp.float32
         )
-        first, last = start // tokens, (start + wide_second) // tokens
-        out_ref[first:last, 0 : tokens // 2] = mixed.T.reshape(last - first, tokens // 2, 2, LANES)
+        mixed = mixed.T
+        for source in range(start // tokens, (start + wide_second) // tokens):
+            out_rows[source, 0:tokens, :] = mixed[source * tokens - start : (source + 1) * tokens - start, :]
     lines = jnp.concatenate([high_line, low_line], axis=0)
     out_ref[:, tokens // 2] = jnp.broadcast_to(lines[None], (sources, EXTRA, LANES))
 
@@ -407,13 +408,9 @@
     mine = lane == (me % per_chunk) * tokens + me // per_chunk
     ratios = jnp.concatenate([jnp.where(mine, jnp.exp(c - page_lse), 0.0) for c in chip_lse], axis=0)
     ratios = jnp.broadcast_to(jnp.sum(ratios, axis=1, keepdims=True), ratios.shape)
-    grad_q = jnp.zeros((tokens // 2, 2, LANES), jnp.float32)
-    for i, s in enumerate(even):
-        grad_q = grad_q + ratios[i : i + 1, :][None] * got_ref[s, 0 : tokens // 2]
-    for s in odd:
-        grad_q = grad_q - got_ref[s, 0 : tokens // 2]
-    for pair in range(tokens // 2):
-        grad_q_ref[0, 2 * pair : 2 * pair + 2, :] = grad_q[pair]
+    got_rows = got_ref.reshape(sources, tokens + EXTRA, LANES)
+    terms = [ratios[i : i + 1, :] * got_rows[s, 0:tokens, :] for i, s in enumerate(even)]
+    grad_q_ref[0] = tree(jnp.add, terms) - tree(jnp.add, [got_rows[s, 0:tokens, :] for s in odd])
     copies.append(pltpu.make_async_copy(grad_q_ref, grad_q_out, sems.at[local_pages]))
     copies[-1].start()
 
@@ -446,18 +443,17 @@
     message = pl.pallas_call(
         first_kernel,
         out_shape=jax.ShapeDtypeStruct((devices, pairs, 2, LANES), jnp.bfloat16),
-        in_specs=[anywhere] * 4,
-        out_specs=anywhere,
+        in_specs=[vmem] + [pl.BlockSpec(memory_space=pltpu.HBM)] * 3,
+        out_specs=vmem,
+        compiler_params=params,
         scratch_shapes=[
-            pltpu.SMEM(positive.shape, jnp.int32),
             pltpu.VMEM(queries.shape, jnp.bfloat16),
             pltpu.VMEM(query_mask.shape, jnp.int32),
             pltpu.VMEM(page_mask.shape, jnp.int32),
-            pltpu.VMEM((devices, pairs, 2, LANES), jnp.bfloat16),
-            pltpu.SemaphoreType.DMA((4,)),
-            pltpu.SemaphoreType.DMA,
+            pltpu.SemaphoreType.DMA((3,)),
         ],
-    )(positive, queries, query_mask, page_mask)
+    )(positive, *[pltpu.with_memory_space_constraint(a, pltpu.HBM) for a in (queries, query_mask, page_mask)])
+    message, other_vectors = lax.optimization_barrier((message, other_vectors))
     sent = exchange(message)
     out, powers, stats, rows_q = pl.pallas_call(
         functools.partial(middle_kernel, tokens),

time: 31.1 us -> 30.4 us (0.977)
  blocking collectives: 10.3 us -> 25 us
  waiting for transfers between devices: 7.57 us -> 0.01 us
  starting transfers between devices: 7.65 us -> 0.56 us
  Pallas kernels: 3.78 us -> 3.1 us
    all_to_all x1 -> x2, blocking collectives: 10.3 us -> 25 us  [exchange(): return lax.all_to_all(blocks_to_all, ('blk', 'group'), 0, 0, tiled=True)]
    all_to_all x1 -> x0, starting transfers between devices: 7.33 us -> none  [exchange(): return lax.all_to_all(blocks_to_all, ('blk', 'group'), 0, 0, tiled=True)]
    all_to_all x1 -> x0, waiting for transfers between devices: 6.56 us -> none  [exchange(): return lax.all_to_all(blocks_to_all, ('blk', 'group'), 0, 0, tiled=True)]
    ppermute x1, waiting for transfers between devices: 1 us -> 0.01 us  [two_exchanges(): other_vectors = lax.ppermute(page_vectors, 'blk', swap)]
    pallas_call x1, Pallas kernels: 1.5 us -> 0.85 us  [two_exchanges(): pl.pallas_call(first_kernel, out_shape=jax.ShapeDtypeStruct((devices, pai...]
  transfers between devices with their start and end apart: 2 -> 1, of which waited for: 2 -> 0; matrix products, arithmetic and copies ran while one was open for 0% -> 0% of each run, Pallas kernels for 0% -> 3%
where the time goes in v4:
time: 30.4 us; the launch traced here: 30.2 us
  blocking collectives  25 us (82%)
  Pallas kernels  3.1 us (10%)
  between operations  1.33 us (4%)
  starting transfers between devices  0.56 us (2%)
    all_to_all x2, blocking collectives, exchange(): return lax.all_to_all(blocks_to_all, ('blk', 'group'), 0, 0, tiled=True)  25 us
    pallas_call x1, Pallas kernels, two_exchanges(): pl.pallas_call(functools.partial(middle_kernel, tokens), out_shape=(jax.S...  1.25 us
    pallas_call x1, Pallas kernels, two_exchanges(): pl.pallas_call(functools.partial(last_kernel, tokens), out_shape=(jax.Sha...  1 us
    pallas_call x1, Pallas kernels, two_exchanges(): pl.pallas_call(first_kernel, out_shape=jax.ShapeDtypeStruct((devices, pai...  0.85 us
  transfers between devices with their start and end apart: 1, of which 0 were waited for; matrix products, arithmetic and copies ran while one was open for 0% of the time, Pallas kernels for 3%

profile of v4, /device:TPU:0, one launch (start us, length us, event | category | flops | bytes accessed | tf_op | source)
XLA Modules:
  0.0 30.2 jit_solution(8280445351723347107)
XLA Ops:
  0.6 0.6 %collective-permute-start = (bf16[2,128,128]{2,1,0:T(8,128)(2,1)}, bf16[2,128,128]{2,1,0:T(8,128)(2,1)S(1)}, u32[]{:S(2)}, u32[]{:S(2)}) collective-permute-start(bf16[2,128,128]{2,1,0:T(8,128)(2,1)} %own_ref.1), channel_id=1, source_target_pairs={{0,8},{8,0},{16,24},{24,16},{1,9},{9,1},{17,25},{25,17},{2,10},{10... | collective-permute-start | bytes 196616 | tf_op jit(solution)/shard_map/ppermute | solution.py:438
  1.8 0.8 %shard_map.76 = bf16[32,9,2,128]{3,2,1,0:T(2,128)(2,1)S(1)} custom-call(s32[1]{0:T(128)S(6)} %copy.8.target_ref, bf16[1,16,128]{2,1,0:T(8,128)(2,1)} %queries_ref.1, s32[1,16]{1,0:T(1,128)} %query_mask_ref.1, s32[2,128]{1,0:T(2,128)} %page_mask_ref.1), custom_call_target="tpu_custom_call" | custom-call | tf_op jit(solution)/shard_map/pallas_call | solution.py:443
  2.7 0.0 copy-start
  2.7 0.0 collective-permute-done.other_ref
  2.7 14.7 %all_to_all.10.sent_ref = bf16[32,9,2,128]{3,2,1,0:T(2,128)(2,1)S(1)} all-to-all(bf16[32,9,2,128]{3,2,1,0:T(2,128)(2,1)S(1)} %shard_map.76), channel_id=1, replica_groups=mesh['blk'=4,'group'=8] {'blk','group'}, dimensions={0} | all-to-all | bytes 294912 | tf_op jit(solution)/shard_map/all_to_all | solution.py:427
  17.4 0.0 copy-done
  17.4 1.3 %shard_map.77 = (f32[32,9,2,128]{3,2,1,0:T(2,128)S(1)}, f32[2,128,512]{2,1,0:T(8,128)S(1)}, f32[6,512]{1,0:T(8,128)S(1)}, bf16[512,128]{1,0:T(8,128)(2,1)S(1)}) custom-call(bf16[32,9,2,128]{3,2,1,0:T(2,128)(2,1)S(1)} %all_to_all.10.sent_ref, bf16[2,128,128]{2,1,0:T(8,128)(2,1)S(1)} %copy-done, bf16[2,128,128]{2,1,0:T(8,128)(2,1)S(1)} %collective-permute-done.other_ref), custom_call_target="tpu_custom_call" | custom-call | tf_op jit(solution)/shard_map/pallas_call | solution.py:458
  18.6 0.1 convert_element_type.6
  18.7 10.3 %all_to_all.11 = f16[32,9,2,128]{3,2,1,0:T(2,128)(2,1)S(1)} all-to-all(f16[32,9,2,128]{3,2,1,0:T(2,128)(2,1)S(1)} %convert_element_type.6), channel_id=1, replica_groups=mesh['blk'=4,'group'=8] {'blk','group'}, dimensions={0} | all-to-all | bytes 294912 | tf_op jit(solution)/shard_map/all_to_all | solution.py:427
  29.1 0.1 convert_element_type.7.got_ref
  29.2 1.0 %shard_map.78 = (f32[1,16,128]{2,1,0:T(8,128)}, f32[2,128,128]{2,1,0:T(8,128)}, f32[1,1]{1,0:T(1,128)}) custom-call(f32[32,9,2,128]{3,2,1,0:T(2,128)S(1)} %convert_element_type.7.got_ref, bf16[512,128]{1,0:T(8,128)(2,1)S(1)} %get-tuple-element.15.rows_ref, f32[2,128,512]{2,1,0:T(8,128)S(1)} %get-tuple-element.16.power_ref, ...), custom_call_target="tpu_custom_call" | custom-call | tf_op jit(solution)/shard_map/pallas_call | solution.py:472
Async XLA Ops:
  0.6 2.1 %collective-permute-start = (bf16[2,128,128]{2,1,0:T(8,128)(2,1)}, bf16[2,128,128]{2,1,0:T(8,128)(2,1)S(1)}, u32[]{:S(2)}, u32[]{:S(2)}) collective-permute-start(bf16[2,128,128]{2,1,0:T(8,128)(2,1)} %own_ref.1), channel_id=1, source_target_pairs={{0,8},{8,0},{16,24},{24,16},{1,9},{9,1},{17,25},{25,17},{2,10},{10... | collective-permute-start | bytes 196616 | tf_op jit(solution)/shard_map/ppermute | solution.py:438
  2.7 14.7 %copy-start = (bf16[2,128,128]{2,1,0:T(8,128)(2,1)S(1)}, bf16[2,128,128]{2,1,0:T(8,128)(2,1)}, u32[]{:S(2)}) copy-start(bf16[2,128,128]{2,1,0:T(8,128)(2,1)} %own_ref.1) | copy-start | bytes 196612

commit v5 on v4

--- a/solution.py
+++ b/solution.py
@@ -183,8 +183,6 @@
 LANES = 128
 EXTRA = 2
 FACTS = 16
-WIDE_FIRST = 256
-WIDE_SECOND = 256
 KERNEL_VMEM = 16 * 2**20
 
 
@@ -230,7 +228,8 @@
 def first_kernel(target_ref, queries_ref, query_mask_ref, page_mask_ref, out_ref, *scratch):
     queries, query_mask, page_mask, sems = scratch
     devices = out_ref.shape[0]
-    tokens = queries_ref.shape[1]
+    half = queries_ref.shape[1] // 2
+    members = lax.axis_size("group")
     loads = [
         pltpu.make_async_copy(src, dst, sems.at[i])
         for i, (src, dst) in enumerate(
@@ -246,7 +245,7 @@
     for load in loads:
         load.wait()
     alive = jnp.sum(query_mask[...].astype(jnp.float32), axis=1, keepdims=True)
-    kind = lax.broadcasted_iota(jnp.int32, (EXTRA, LANES), 1) % FACTS
+    kind = lax.broadcasted_iota(jnp.int32, (EXTRA, LANES), 1) % half
     number = target_ref[...].reshape(1, 1)
     facts = jnp.where(kind == 0, alive, 0.0)
     facts = jnp.where(kind == 1, (number >> 8).astype(jnp.float32), facts)
@@ -254,124 +253,169 @@
     for page in range(page_mask.shape[0]):
         count = jnp.sum(page_mask[page : page + 1, :].astype(jnp.float32), axis=1, keepdims=True)
         facts = jnp.where(kind == 3 + page, count, facts)
-    out_rows = out_ref.reshape(devices, tokens + EXTRA, LANES)
+    out_rows = out_ref.reshape(devices, half + EXTRA, LANES)
     for device in range(devices):
-        out_rows[device, 0:tokens, :] = queries[0]
-    out_ref[:, tokens // 2] = jnp.broadcast_to(facts.astype(jnp.bfloat16)[None], (devices, EXTRA, LANES))
-
-
-def middle_kernel(tokens, sent_ref, own_ref, other_ref, out_ref, power_ref, stat_ref, rows_ref, other_power_ref):
+        begin = (device // members) % 2 * half
+        out_rows[device, 0:half, :] = queries[0, begin : begin + half, :]
+    out_ref[:, half // 2] = jnp.broadcast_to(facts.astype(jnp.bfloat16)[None], (devices, EXTRA, LANES))
+
+
+def measure_pages(rows_q, vectors, flips, counts, alive, powers_ref=None):
+    width = rows_q.shape[0]
+    patch = lax.broadcasted_iota(jnp.int32, (LANES, width), 0).astype(jnp.float32)
+    steep = 1.0 / (relaxation_scale_factor * math.log(2.0))
+    softened, inverses, mixes = [], [], []
+    for page, (block, flipped, count) in enumerate(zip(vectors, flips, counts)):
+        similarity = lax.dot_general(
+            block, rows_q, (((1,), (1,)), ((), ())), preferred_element_type=jnp.float32
+        )
+        masked = jnp.where(patch < count, similarity, guarded_floor_entry)
+        highest = jnp.max(masked, axis=0, keepdims=True)
+        powers = jnp.exp2((masked - highest) * steep)
+        if powers_ref is not None:
+            powers_ref[page] = powers
+        high = powers.astype(jnp.bfloat16)
+        low = (powers - high.astype(jnp.float32)).astype(jnp.bfloat16)
+        mixes.append(
+            jnp.dot(
+                jnp.concatenate([flipped, flipped], axis=1),
+                jnp.concatenate([high, low], axis=0),
+                preferred_element_type=jnp.float32,
+            )
+        )
+        total = jnp.sum(powers, axis=0, keepdims=True)
+        lse = highest * (1.0 / relaxation_scale_factor) + jnp.log(total)
+        softened.append(alive * (relaxation_scale_factor * (lse - jnp.log(count))))
+        inverses.append(alive / total)
+    return softened, inverses, mixes
+
+
+def gather_rows(from_ref, to_ref):
+    sources = from_ref.shape[0]
+    half = 2 * (from_ref.shape[1] - 1)
+    view = from_ref.reshape(sources, half + EXTRA, LANES)
+    for source in range(sources):
+        to_ref[source * half : (source + 1) * half, :] = view[source, 0:half, :]
+
+
+def page_counts(sent_ref, home, local_pages):
+    facts = sent_ref[home, sent_ref.shape[1] - 1].astype(jnp.float32)
+    return [facts[0:1, 3 + number : 4 + number] for number in range(local_pages)]
+
+
+def near_kernel(sent_ref, own_ref, rows_ref, power_ref, soft_ref, inverse_ref, facts_ref, mix_ref, flip_ref):
     sources = sent_ref.shape[0]
-    lanes = sources * tokens
-    chunks = lanes // LANES
-    per_chunk = LANES // tokens
+    half = 2 * (sent_ref.shape[1] - 1)
+    part = sources * half
+    per_chunk = LANES // half
+    local_pages = own_ref.shape[0]
+    blk = lax.axis_index("blk")
+    home = blk * lax.axis_size("group") + lax.axis_index("group")
+    slot = lax.broadcasted_iota(jnp.int32, (1, LANES), 1) // half
+    facts = []
+    for c in range(part // LANES):
+        told = jnp.zeros((1, LANES), jnp.float32)
+        for i in range(per_chunk):
+            told = jnp.where(slot == i, sent_ref[c * per_chunk + i, half // 2, 0:1, :].astype(jnp.float32), told)
+        facts.append(spread_runs(told, half))
+    facts = jnp.concatenate(facts, axis=1)
+    facts_ref[...] = facts
+    token = lax.broadcasted_iota(jnp.int32, (1, part), 1) % half + (blk & 1) * half
+    alive = (token.astype(jnp.float32) < facts[0:1]).astype(jnp.float32)
+    gather_rows(sent_ref, rows_ref)
+    vectors = [own_ref[page] for page in range(local_pages)]
+    flips = [block.T for block in vectors]
+    softened, inverses, mixes = measure_pages(
+        rows_ref[...], vectors, flips, page_counts(sent_ref, home, local_pages), alive, power_ref
+    )
+    for page in range(local_pages):
+        mix_ref[page] = mixes[page]
+        flip_ref[page] = flips[page]
+        soft_ref[page : page + 1, :] = softened[page]
+        inverse_ref[page : page + 1, :] = inverses[page]
+
+
+def far_kernel(*refs):
+    sent_ref, swapped_ref, own_ref, other_ref, near_rows_ref, near_mix_ref, near_soft_ref, near_inverse_ref = refs[:8]
+    facts_ref, flip_ref, out_ref, power_ref, score_ref, inverse_ref, rows_ref = refs[8:]
+    sources = sent_ref.shape[0]
+    half = 2 * (sent_ref.shape[1] - 1)
+    part = sources * half
     local_pages = own_ref.shape[0]
     blk = lax.axis_index("blk")
     group = lax.axis_index("group")
     members = lax.axis_size("group")
     homes = [blk * members + group, (blk ^ 1) * members + group]
-    sends_sum = (blk & 1) == 0
-
-    counts, ids, vectors, powers_refs = [], [], [], []
-    for vectors_ref, kept_ref, home in ((own_ref, power_ref, homes[0]), (other_ref, other_power_ref, homes[1])):
-        facts = sent_ref[home, tokens // 2].astype(jnp.float32)
-        for number in range(local_pages):
-            counts.append(facts[0:1, 3 + number : 4 + number])
-            ids.append(home * local_pages + number)
-            vectors.append(vectors_ref[number])
-            powers_refs.append(kept_ref.at[number])
-    slot = lax.broadcasted_iota(jnp.int32, (1, LANES), 1) // tokens
-    spot = lax.broadcasted_iota(jnp.int32, (1, LANES), 1) % tokens
-    sent_rows = sent_ref.reshape(sources, tokens + EXTRA, LANES)
-    out_rows = out_ref.reshape(sources, tokens + EXTRA, LANES)
-    steep = 1.0 / (relaxation_scale_factor * math.log(2.0))
-
-    scales = []
+    side = blk & 1
+    sends_sum = side == 0
+    own_range = range(local_pages)
+    ids = [home * local_pages + page for home in homes for page in own_range]
+    own = [own_ref[page] for page in own_range]
+    other = [other_ref[page] for page in own_range]
+    own_flips = [flip_ref[page] for page in own_range]
+    other_flips = [block.T for block in other]
+    own_counts = page_counts(sent_ref, homes[0], local_pages)
+    other_counts = page_counts(sent_ref, homes[1], local_pages)
+
+    facts = facts_ref[...]
+    target = (facts[1:2] * 256.0 + facts[2:3]).astype(jnp.int32)
+    spot = lax.broadcasted_iota(jnp.int32, (1, part), 1) % half
+    near_alive = ((spot + side * half).astype(jnp.float32) < facts[0:1]).astype(jnp.float32)
+    far_alive = ((spot + (1 - side) * half).astype(jnp.float32) < facts[0:1]).astype(jnp.float32)
+    other_soft, other_inverse, other_mix = measure_pages(near_rows_ref[...], other, other_flips, other_counts, near_alive)
+    gather_rows(swapped_ref, rows_ref)
+    rows_q = rows_ref[...]
+    far_soft, far_inverse, far_mix = measure_pages(rows_q, own, own_flips, own_counts, far_alive, power_ref)
+    cross_soft, cross_inverse, cross_mix = measure_pages(rows_q, other, other_flips, other_counts, far_alive)
+    near_mix = [near_mix_ref[page] for page in own_range]
+    near_soft = [near_soft_ref[page : page + 1, :] for page in own_range]
+    near_inverse = [near_inverse_ref[page : page + 1, :] for page in own_range]
+    for page in own_range:
+        inverse_ref[page : page + 1, :] = far_inverse[page]
+    softened = [a + b for a, b in zip(near_soft + other_soft, far_soft + cross_soft)]
+    scores = segment_sum(jnp.concatenate(softened, axis=0), half)
+    top = jnp.max(scores, axis=0, keepdims=True)
+    chip_lse = top + jnp.log(jnp.sum(jnp.exp(scores - top), axis=0, keepdims=True))
+
+    picked = jnp.zeros((1, part), jnp.float32)
+    shares = []
+    for page, name in enumerate(ids):
+        score = scores[page : page + 1]
+        hit = target == name
+        picked = picked + jnp.where(hit, score, 0.0)
+        shares.append(jnp.where(sends_sum, jnp.exp(score - chip_lse), hit.astype(jnp.float32)))
+        if page < local_pages:
+            score_ref[page : page + 1, :] = score
+            score_ref[local_pages + page : local_pages + page + 1, :] = hit.astype(jnp.float32)
+    high, low = split_half(jnp.where(sends_sum, chip_lse, picked))
     high_line = jnp.zeros((1, LANES), jnp.float32)
     low_line = jnp.zeros((1, LANES), jnp.float32)
-    wide_first = math.gcd(WIDE_FIRST, lanes)
-    for start in range(0, lanes, wide_first):
-        columns = pl.ds(start, wide_first)
-        facts = []
-        for c in range(start // LANES, (start + wide_first) // LANES):
-            told = jnp.zeros((1, LANES), jnp.float32)
-            for i in range(per_chunk):
-                told = jnp.where(
-                    slot == i, sent_ref[c * per_chunk + i, tokens // 2, 0:1, :].astype(jnp.float32), told
-                )
-            facts.append(spread_runs(told, tokens))
-        facts = jnp.concatenate(facts, axis=1)
-        spots = lax.broadcasted_iota(jnp.int32, (1, wide_first), 1) % tokens
-        alive = (spots.astype(jnp.float32) < facts[0:1]).astype(jnp.float32)
-        target = (facts[1:2] * 256.0 + facts[2:3]).astype(jnp.int32)
-        first, last = start // tokens, (start + wide_first) // tokens
-        for source in range(first, last):
-            rows_ref[source * tokens : (source + 1) * tokens, :] = sent_rows[source, 0:tokens, :]
-        rows_q = rows_ref[columns, :]
-
-        softened, inverses = [], []
-        patch = lax.broadcasted_iota(jnp.int32, (LANES, wide_first), 0).astype(jnp.float32)
-        for page in range(2 * local_pages):
-            similarity = lax.dot_general(
-                vectors[page], rows_q, (((1,), (1,)), ((), ())), preferred_element_type=jnp.float32
-            )
-            masked = jnp.where(patch < counts[page], similarity, guarded_floor_entry)
-            highest = jnp.max(masked, axis=0, keepdims=True)
-            powers = jnp.exp2((masked - highest) * steep)
-            powers_refs[page][:, columns] = powers
-            total = jnp.sum(powers, axis=0, keepdims=True)
-            lse = highest * (1.0 / relaxation_scale_factor) + jnp.log(total)
-            softened.append(alive * (relaxation_scale_factor * (lse - jnp.log(counts[page]))))
-            inverses.append(alive / total)
-        scores = segment_sum(jnp.concatenate(softened, axis=0), tokens)
-        top = jnp.max(scores, axis=0, keepdims=True)
-        chip_lse = top + jnp.log(jnp.sum(jnp.exp(scores - top), axis=0, keepdims=True))
-
-        picked = jnp.zeros((1, wide_first), jnp.float32)
-        chunk_scales = []
-        for page in range(2 * local_pages):
-            score = scores[page : page + 1]
-            hit = target == ids[page]
-            picked = picked + jnp.where(hit, score, 0.0)
-            share = jnp.where(sends_sum, jnp.exp(score - chip_lse), hit.astype(jnp.float32))
-            chunk_scales.append(inverses[page] * share)
-            if page < local_pages:
-                for row, value in enumerate((score, hit.astype(jnp.float32), inverses[page])):
-                    stat_ref[row * local_pages + page : row * local_pages + page + 1, columns] = value
-        scales.append(chunk_scales)
-        high, low = split_half(jnp.where(sends_sum, chip_lse, picked))
-        for offset in range(0, wide_first, LANES):
-            c = (start + offset) // LANES
-            high_line = jnp.where(spot == c, high[:, offset : offset + LANES], high_line)
-            low_line = jnp.where(spot == c, low[:, offset : offset + LANES], low_line)
-
-    scales = [jnp.concatenate([part[page] for part in scales], axis=1) for page in range(2 * local_pages)]
-    flipped = jnp.concatenate(vectors, axis=0).T
-    wide_second = math.gcd(WIDE_SECOND, lanes)
-    for start in range(0, lanes, wide_second):
-        highs, lows = [], []
-        for page in range(2 * local_pages):
-            term = powers_refs[page][:, pl.ds(start, wide_second)] * scales[page][:, start : start + wide_second]
-            high = term.astype(jnp.bfloat16)
-            highs.append(high)
-            lows.append((term - high.astype(jnp.float32)).astype(jnp.bfloat16))
-        mixed = jnp.dot(flipped, jnp.concatenate(highs, axis=0), preferred_element_type=jnp.float32) + jnp.dot(
-            flipped, jnp.concatenate(lows, axis=0), preferred_element_type=jnp.float32
-        )
+    for c in range(part // LANES):
+        high_line = jnp.where(spot[:, 0:LANES] == c, high[:, c * LANES : (c + 1) * LANES], high_line)
+        low_line = jnp.where(spot[:, 0:LANES] == c, low[:, c * LANES : (c + 1) * LANES], low_line)
+    lines = jnp.concatenate([high_line, low_line], axis=0)
+    out_ref[:, half] = jnp.broadcast_to(lines[None], (sources, EXTRA, LANES))
+
+    out_rows = out_ref.reshape(sources, 2 * half + EXTRA, LANES)
+    for position, (mixes, inverses) in enumerate(
+        ((near_mix + other_mix, near_inverse + other_inverse), (far_mix + cross_mix, far_inverse + cross_inverse))
+    ):
+        mixed = sum(mix * (inverse * share) for mix, inverse, share in zip(mixes, inverses, shares))
         mixed = mixed.T
-        for source in range(start // tokens, (start + wide_second) // tokens):
-            out_rows[source, 0:tokens, :] = mixed[source * tokens - start : (source + 1) * tokens - start, :]
-    lines = jnp.concatenate([high_line, low_line], axis=0)
-    out_ref[:, tokens // 2] = jnp.broadcast_to(lines[None], (sources, EXTRA, LANES))
-
-
-def last_kernel(tokens, got_ref, rows_ref, power_ref, stat_ref, grad_q_out, grad_p_out, loss_out, *scratch):
-    grad_q_ref, grad_p_ref, loss_ref, sems = scratch
+        for source in range(sources):
+            out_rows[source, position * half : (position + 1) * half, :] = mixed[
+                source * half : (source + 1) * half, :
+            ]
+
+
+def last_kernel(tokens, got_ref, score_ref, *rest):
+    near, far, results = rest[0:3], rest[3:6], rest[6:]
+    grad_q_out, grad_p_out, loss_out, grad_q_ref, grad_p_ref, loss_ref, sems = results
     sources = got_ref.shape[0]
-    lanes = sources * tokens
-    chunks = lanes // LANES
-    per_chunk = LANES // tokens
-    local_pages = power_ref.shape[0]
+    half = tokens // 2
+    chunks = sources * half // LANES
+    per_chunk = LANES // half
+    local_pages = grad_p_ref.shape[0]
     blk = lax.axis_index("blk")
     group = lax.axis_index("group")
     members = lax.axis_size("group")
@@ -390,32 +434,36 @@
     chip_lse = [stats(s) for s in even]
     top = tree(jnp.maximum, chip_lse)
     page_lse = top + jnp.log(tree(jnp.add, [jnp.exp(c - top) for c in chip_lse]))
-    spread = spread_runs(page_lse, tokens)
+    spread = spread_runs(page_lse, half)
     flat = jnp.concatenate([spread[c : c + 1] for c in range(chunks)], axis=1)
-    rows_q = rows_ref[...]
     copies = []
     for page in range(local_pages):
-        score, hit, inverse = (
-            stat_ref[row * local_pages + page : row * local_pages + page + 1, :] for row in range(3)
-        )
-        coefficient = (jnp.exp(score - flat) - hit) * inverse
-        factor = (coefficient * power_ref[page]).astype(jnp.bfloat16)
-        grad_p_ref[page] = jnp.dot(factor, rows_q, preferred_element_type=jnp.float32)
+        score = score_ref[page : page + 1, :]
+        hit = score_ref[local_pages + page : local_pages + page + 1, :]
+        coefficient = jnp.exp(score - flat) - hit
+        grad_p = jnp.zeros((LANES, LANES), jnp.float32)
+        for rows_ref, power_ref, inverse_ref in (near, far):
+            factor = (coefficient * inverse_ref[page : page + 1, :] * power_ref[page]).astype(jnp.bfloat16)
+            grad_p += jnp.dot(factor, rows_ref[...], preferred_element_type=jnp.float32)
+        grad_p_ref[page] = grad_p
         copies.append(pltpu.make_async_copy(grad_p_ref.at[page], grad_p_out.at[page], sems.at[page]))
         copies[-1].start()
 
     lane = lax.broadcasted_iota(jnp.int32, (1, LANES), 1)
-    mine = lane == (me % per_chunk) * tokens + me // per_chunk
+    mine = lane == (me % per_chunk) * half + me // per_chunk
     ratios = jnp.concatenate([jnp.where(mine, jnp.exp(c - page_lse), 0.0) for c in chip_lse], axis=0)
     ratios = jnp.broadcast_to(jnp.sum(ratios, axis=1, keepdims=True), ratios.shape)
     got_rows = got_ref.reshape(sources, tokens + EXTRA, LANES)
     terms = [ratios[i : i + 1, :] * got_rows[s, 0:tokens, :] for i, s in enumerate(even)]
-    grad_q_ref[0] = tree(jnp.add, terms) - tree(jnp.add, [got_rows[s, 0:tokens, :] for s in odd])
+    sums = tree(jnp.add, terms)
+    single = tree(jnp.add, [got_rows[s, 0:tokens, :] for s in odd])
+    grad_q_ref[0, 0:half, :] = sums[0:half] - single[half:tokens]
+    grad_q_ref[0, half:tokens, :] = sums[half:tokens] - single[0:half]
     copies.append(pltpu.make_async_copy(grad_q_ref, grad_q_out, sems.at[local_pages]))
     copies[-1].start()
 
     picked = tree(jnp.add, [stats(s) for s in odd])
-    difference = jnp.where(lane % tokens < chunks, page_lse - picked, 0.0)
+    difference = jnp.where(lane % half < chunks, page_lse - picked, 0.0)
     loss_ref[...] = jnp.sum(difference, axis=1, keepdims=True) * (1.0 / sources)
     copies.append(pltpu.make_async_copy(loss_ref, loss_out, sems.at[local_pages + 1]))
     copies[-1].start()
@@ -433,16 +481,16 @@
     devices = lax.axis_size("blk") * lax.axis_size("group")
     lanes = devices * tokens
     blocks = lax.axis_size("blk")
+    half = tokens // 2
     pairs = (tokens + EXTRA) // 2
     swap = [(b, b ^ 1) for b in range(blocks)]
-    other_vectors = lax.ppermute(page_vectors, "blk", swap)
 
     vmem = pl.BlockSpec(memory_space=pltpu.VMEM)
     anywhere = pl.BlockSpec(memory_space=pl.ANY)
     params = pltpu.CompilerParams(vmem_limit_bytes=KERNEL_VMEM)
     message = pl.pallas_call(
         first_kernel,
-        out_shape=jax.ShapeDtypeStruct((devices, pairs, 2, LANES), jnp.bfloat16),
+        out_shape=jax.ShapeDtypeStruct((devices, (half + EXTRA) // 2, 2, LANES), jnp.bfloat16),
         in_specs=[vmem] + [pl.BlockSpec(memory_space=pltpu.HBM)] * 3,
         out_specs=vmem,
         compiler_params=params,
@@ -453,21 +501,37 @@
             pltpu.SemaphoreType.DMA((3,)),
         ],
     )(positive, *[pltpu.with_memory_space_constraint(a, pltpu.HBM) for a in (queries, query_mask, page_mask)])
-    message, other_vectors = lax.optimization_barrier((message, other_vectors))
     sent = exchange(message)
-    out, powers, stats, rows_q = pl.pallas_call(
-        functools.partial(middle_kernel, tokens),
+    sent, page_vectors = lax.optimization_barrier((sent, page_vectors))
+    swapped = lax.ppermute(sent, "blk", swap)
+    other_vectors = lax.ppermute(page_vectors, "blk", swap)
+    part = lanes // 2
+    kept = (
+        jax.ShapeDtypeStruct((part, LANES), jnp.bfloat16),
+        jax.ShapeDtypeStruct((local_pages, LANES, part), jnp.float32),
+        jax.ShapeDtypeStruct((local_pages, part), jnp.float32),
+    )
+    near_rows, near_powers, near_soft, near_inverses, facts, near_mix, flips = pl.pallas_call(
+        near_kernel,
+        out_shape=kept + (kept[2], jax.ShapeDtypeStruct((8, part), jnp.float32), kept[1], jax.ShapeDtypeStruct(page_vectors.shape, jnp.bfloat16)),
+        in_specs=[vmem] * 2,
+        out_specs=(vmem,) * 7,
+        compiler_params=params,
+        cost_estimate=pl.CostEstimate(flops=4 * part * LANES * LANES, bytes_accessed=2**20, transcendentals=part * LANES),
+    )(sent, page_vectors)
+    out, far_powers, scores, far_inverses, far_rows = pl.pallas_call(
+        far_kernel,
         out_shape=(
             jax.ShapeDtypeStruct((devices, pairs, 2, LANES), jnp.float32),
-            jax.ShapeDtypeStruct((local_pages, LANES, lanes), jnp.float32),
-            jax.ShapeDtypeStruct((3 * local_pages, lanes), jnp.float32),
-            jax.ShapeDtypeStruct((lanes, LANES), jnp.bfloat16),
+            kept[1],
+            jax.ShapeDtypeStruct((2 * local_pages, part), jnp.float32),
+            kept[2],
+            kept[0],
         ),
-        in_specs=[vmem] * 3,
-        out_specs=(vmem,) * 4,
-        scratch_shapes=[pltpu.VMEM((local_pages, LANES, lanes), jnp.float32)],
+        in_specs=[vmem] * 10,
+        out_specs=(vmem,) * 5,
         compiler_params=params,
-    )(sent, page_vectors, other_vectors)
+    )(sent, swapped, page_vectors, other_vectors, near_rows, near_mix, near_soft, near_inverses, facts, flips)
     got = exchange(out.astype(jnp.float16)).astype(jnp.float32)
     grad_q, grad_p, loss = pl.pallas_call(
         functools.partial(last_kernel, tokens),
@@ -476,7 +540,7 @@
             jax.ShapeDtypeStruct(page_vectors.shape, jnp.float32),
             jax.ShapeDtypeStruct((1, 1), jnp.float32),
         ),
-        in_specs=[vmem] * 4,
+        in_specs=[vmem] * 8,
         out_specs=(anywhere,) * 3,
         scratch_shapes=[
             pltpu.VMEM(queries.shape, jnp.float32),
@@ -485,7 +549,7 @@
             pltpu.SemaphoreType.DMA((local_pages + 2,)),
         ],
         compiler_params=params,
-    )(got, rows_q, powers, stats)
+    )(got, scores, near_rows, near_powers, near_inverses, far_rows, far_powers, far_inverses)
     return (grad_q, grad_p, loss[0, 0])
 
 

time: 30.4 us -> 30.1 us (level)
  blocking collectives: 25 us -> 24.1 us
  waiting for transfers between devices: 0.01 us -> 0.45 us
    all_to_all x2, blocking collectives: 25 us -> 24.1 us  [exchange(): return lax.all_to_all(blocks_to_all, ('blk', 'group'), 0, 0, tiled=True)]
    ppermute x1, waiting for transfers between devices: 0.01 us -> 0.44 us  [two_exchanges(): other_vectors = lax.ppermute(page_vectors, 'blk', swap)]
    pallas_call x2 -> x3, Pallas kernels: 2.1 us -> 2.2 us  [the longest x1 0.9 us: two_exchanges(): pl.pallas_call(far_kernel, out_shape=(jax.ShapeDtypeStruct((devices, pair...]
  transfers between devices with their start and end apart: 1 -> 2, of which waited for: 0 -> 1; matrix products, arithmetic and copies ran while one was open for 0% -> 0% of each run, Pallas kernels for 3% -> 2%
where the time goes in v5:
time: 30.1 us; the launch traced here: 29.9 us
  blocking collectives  24.1 us (80%)
  Pallas kernels  3.21 us (11%)
  between operations  1.32 us (4%)
  starting transfers between devices  0.51 us (2%)
  waiting for transfers between devices  0.45 us (1%)
    all_to_all x2, blocking collectives, exchange(): return lax.all_to_all(blocks_to_all, ('blk', 'group'), 0, 0, tiled=True)  24.1 us
    pallas_call x1, Pallas kernels, two_exchanges(): pl.pallas_call(functools.partial(last_kernel, tokens), out_shape=(jax.Sha...  1.02 us
    pallas_call x1, Pallas kernels, two_exchanges(): pl.pallas_call(far_kernel, out_shape=(jax.ShapeDtypeStruct((devices, pair...  0.9 us
    pallas_call x1, Pallas kernels, two_exchanges(): pl.pallas_call(first_kernel, out_shape=jax.ShapeDtypeStruct((devices, (ha...  0.85 us
  transfers between devices with their start and end apart: 2, of which 1 were waited for; matrix products, arithmetic and copies ran while one was open for 0% of the time, Pallas kernels for 2%

profile of v5, /device:TPU:0, one launch (start us, length us, event | category | flops | bytes accessed | tf_op | source)
XLA Modules:
  0.0 29.9 jit_solution(12128325243766023157)
XLA Ops:
  1.3 0.8 %shard_map.76 = bf16[32,5,2,128]{3,2,1,0:T(2,128)(2,1)S(1)} custom-call(s32[1]{0:T(128)S(6)} %copy.8.target_ref, bf16[1,16,128]{2,1,0:T(8,128)(2,1)} %queries_ref.1, s32[1,16]{1,0:T(1,128)} %query_mask_ref.1, s32[2,128]{1,0:T(2,128)} %page_mask_ref.1), custom_call_target="tpu_custom_call" | custom-call | tf_op jit(solution)/shard_map/pallas_call | solution.py:491
  2.1 0.0 copy-start
  2.1 14.5 %all_to_all.10.sent_ref.refs_0_ = bf16[32,5,2,128]{3,2,1,0:T(2,128)(2,1)S(1)} all-to-all(bf16[32,5,2,128]{3,2,1,0:T(2,128)(2,1)S(1)} %shard_map.76), channel_id=1, replica_groups=mesh['blk'=4,'group'=8] {'blk','group'}, dimensions={0} | all-to-all | bytes 163840 | tf_op jit(solution)/shard_map/all_to_all | solution.py:475
  16.7 0.1 collective-permute-start
  16.8 0.0 copy-done
  16.8 0.4 %collective-permute-start.1 = (bf16[2,128,128]{2,1,0:T(8,128)(2,1)S(1)}, bf16[2,128,128]{2,1,0:T(8,128)(2,1)S(1)}, u32[]{:S(2)}, u32[]{:S(2)}) collective-permute-start(bf16[2,128,128]{2,1,0:T(8,128)(2,1)S(1)} %copy-done), channel_id=1, source_target_pairs={{0,8},{8,0},{16,24},{24,16},{1,9},{9,1},{17,25},{25,17},{2,10},{10... | collective-permute-start | bytes 196616 | tf_op jit(solution)/shard_map/ppermute | solution.py:507
  17.2 0.5 %shard_map.77 = (bf16[256,128]{1,0:T(8,128)(2,1)S(1)}, f32[2,128,256]{2,1,0:T(8,128)S(1)}, f32[2,256]{1,0:T(2,128)S(1)}, f32[2,256]{1,0:T(2,128)S(1)}, f32[8,256...) custom-call(bf16[32,5,2,128]{3,2,1,0:T(2,128)(2,1)S(1)} %all_to_all.10.sent_ref.refs_0_, ...), custom_call_target="tpu_custom_call" | custom-call | flops 16777216 | bytes 1048576 | tf_op jit(solution)/shard_map/pallas_call | solution.py:514
  17.7 0.4 %collective-permute-done.1.refs_3_ = bf16[2,128,128]{2,1,0:T(8,128)(2,1)S(1)} collective-permute-done((bf16[2,128,128]{2,1,0:T(8,128)(2,1)S(1)}, bf16[2,128,128]{2,1,0:T(8,128)(2,1)S(1)}, u32[]{:S(2)}, u32[]{:S(2)}) %collective-permute-start.1) | collective-permute-done | bytes 65568 | tf_op jit(solution)/shard_map/ppermute | solution.py:507
  18.1 0.0 collective-permute-done.refs_1_
  18.1 0.9 %shard_map.78 = (f32[32,9,2,128]{3,2,1,0:T(2,128)S(1)}, f32[2,128,256]{2,1,0:T(8,128)S(1)}, f32[4,256]{1,0:T(4,128)S(1)}, f32[2,256]{1,0:T(2,128)S(1)}, bf16[256,128]{1,0:T(8,128)(2,1)S(1)}) custom-call(bf16[32,5,2,128]{3,2,1,0:T(2,128)(2,1)S(1)} %all_to_all.10.sent_ref.refs_0_, bf16[32,5,2,128]{3,2,1,0:T(2,128)(2,1)S(1)} %collective-permute-done.refs_1_, ...), custom_call_target="tpu_custom_call" | custom-call | tf_op jit(solution)/shard_map/pallas_call | solution.py:522
  19.0 0.1 convert_element_type.6
  19.1 9.6 %all_to_all.11 = f16[32,9,2,128]{3,2,1,0:T(2,128)(2,1)S(1)} all-to-all(f16[32,9,2,128]{3,2,1,0:T(2,128)(2,1)S(1)} %convert_element_type.6), channel_id=1, replica_groups=mesh['blk'=4,'group'=8] {'blk','group'}, dimensions={0} | all-to-all | bytes 294912 | tf_op jit(solution)/shard_map/all_to_all | solution.py:475
  28.7 0.1 convert_element_type.7.got_ref
  28.8 1.0 %shard_map.79 = (f32[1,16,128]{2,1,0:T(8,128)}, f32[2,128,128]{2,1,0:T(8,128)}, f32[1,1]{1,0:T(1,128)}) custom-call(f32[32,9,2,128]{3,2,1,0:T(2,128)S(1)} %convert_element_type.7.got_ref, f32[4,256]{1,0:T(4,128)S(1)} %get-tuple-element.29.score_ref, bf16[256,128]{1,0:T(8,128)(2,1)S(1)} %get-tuple-element.22.refs_4_.rest_0_, ...), custom_call_target="tpu_custom_call" | custom-call | tf_op jit(solution)/shard_map/pallas_call | solution.py:536
Async XLA Ops:
  2.1 14.7 %copy-start = (bf16[2,128,128]{2,1,0:T(8,128)(2,1)S(1)}, bf16[2,128,128]{2,1,0:T(8,128)(2,1)}, u32[]{:S(2)}) copy-start(bf16[2,128,128]{2,1,0:T(8,128)(2,1)} %refs_2_) | copy-start | bytes 196612
  16.7 1.4 %collective-permute-start = (bf16[32,5,2,128]{3,2,1,0:T(2,128)(2,1)S(1)}, bf16[32,5,2,128]{3,2,1,0:T(2,128)(2,1)S(1)}, u32[]{:S(2)}, u32[]{:S(2)}) collective-permute-start(bf16[32,5,2,128]{3,2,1,0:T(2,128)(2,1)S(1)} %all_to_all.10.sent_ref.refs_0_), channel_id=1, source_target_pairs={{0,8},{8,0},{16,24},{24,16},{1,9},{9,1},{17,25},{25,17},{2,10},{10... | collective-permute-start | bytes 245768 | tf_op jit(solution)/shard_map/ppermute | solution.py:506
  16.8 1.3 %collective-permute-start.1 = (bf16[2,128,128]{2,1,0:T(8,128)(2,1)S(1)}, bf16[2,128,128]{2,1,0:T(8,128)(2,1)S(1)}, u32[]{:S(2)}, u32[]{:S(2)}) collective-permute-start(bf16[2,128,128]{2,1,0:T(8,128)(2,1)S(1)} %copy-done), channel_id=1, source_target_pairs={{0,8},{8,0},{16,24},{24,16},{1,9},{9,1},{17,25},{25,17},{2,10},{10... | collective-permute-start | bytes 196616 | tf_op jit(solution)/shard_map/ppermute | solution.py:507

commit v6 on v5

--- a/solution.py
+++ b/solution.py
@@ -184,6 +184,7 @@
 EXTRA = 2
 FACTS = 16
 KERNEL_VMEM = 16 * 2**20
+HALF_SCALE = 2.0**14
 
 
 def fits(queries, page_vectors, devices):
@@ -400,7 +401,7 @@
     for position, (mixes, inverses) in enumerate(
         ((near_mix + other_mix, near_inverse + other_inverse), (far_mix + cross_mix, far_inverse + cross_inverse))
     ):
-        mixed = sum(mix * (inverse * share) for mix, inverse, share in zip(mixes, inverses, shares))
+        mixed = sum(mix * (inverse * (share * HALF_SCALE)) for mix, inverse, share in zip(mixes, inverses, shares))
         mixed = mixed.T
         for source in range(sources):
             out_rows[source, position * half : (position + 1) * half, :] = mixed[
@@ -452,11 +453,12 @@
     lane = lax.broadcasted_iota(jnp.int32, (1, LANES), 1)
     mine = lane == (me % per_chunk) * half + me // per_chunk
     ratios = jnp.concatenate([jnp.where(mine, jnp.exp(c - page_lse), 0.0) for c in chip_lse], axis=0)
-    ratios = jnp.broadcast_to(jnp.sum(ratios, axis=1, keepdims=True), ratios.shape)
+    ratios = jnp.sum(ratios, axis=1, keepdims=True) * (1.0 / HALF_SCALE)
+    ratios = jnp.broadcast_to(ratios, ratios.shape[:1] + (LANES,))
     got_rows = got_ref.reshape(sources, tokens + EXTRA, LANES)
     terms = [ratios[i : i + 1, :] * got_rows[s, 0:tokens, :] for i, s in enumerate(even)]
     sums = tree(jnp.add, terms)
-    single = tree(jnp.add, [got_rows[s, 0:tokens, :] for s in odd])
+    single = tree(jnp.add, [got_rows[s, 0:tokens, :] for s in odd]) * (1.0 / HALF_SCALE)
     grad_q_ref[0, 0:half, :] = sums[0:half] - single[half:tokens]
     grad_q_ref[0, half:tokens, :] = sums[half:tokens] - single[0:half]
     copies.append(pltpu.make_async_copy(grad_q_ref, grad_q_out, sems.at[local_pages]))

time: 30.1 us -> 30.1 us (level)
  no operation moved by 1% of the time
where the time goes in v6:
time: 30.1 us; the launch traced here: 29.9 us
  blocking collectives  24.1 us (80%)
  Pallas kernels  3.21 us (11%)
  between operations  1.32 us (4%)
  starting transfers between devices  0.51 us (2%)
  waiting for transfers between devices  0.45 us (1%)
    all_to_all x2, blocking collectives, exchange(): return lax.all_to_all(blocks_to_all, ('blk', 'group'), 0, 0, tiled=True)  24.1 us
    pallas_call x1, Pallas kernels, two_exchanges(): pl.pallas_call(functools.partial(last_kernel, tokens), out_shape=(jax.Sha...  1.02 us
    pallas_call x1, Pallas kernels, two_exchanges(): pl.pallas_call(far_kernel, out_shape=(jax.ShapeDtypeStruct((devices, pair...  0.9 us
    pallas_call x1, Pallas kernels, two_exchanges(): pl.pallas_call(first_kernel, out_shape=jax.ShapeDtypeStruct((devices, (ha...  0.85 us
  transfers between devices with their start and end apart: 2, of which 1 were waited for; matrix products, arithmetic and copies ran while one was open for 0% of the time, Pallas kernels for 2%

profile of v6, /device:TPU:0, one launch (start us, length us, event | category | flops | bytes accessed | tf_op | source)
XLA Modules:
  0.0 29.9 jit_solution(974672294979062035)
XLA Ops:
  1.3 0.8 %shard_map.76 = bf16[32,5,2,128]{3,2,1,0:T(2,128)(2,1)S(1)} custom-call(s32[1]{0:T(128)S(6)} %copy.8.target_ref, bf16[1,16,128]{2,1,0:T(8,128)(2,1)} %queries_ref.1, s32[1,16]{1,0:T(1,128)} %query_mask_ref.1, s32[2,128]{1,0:T(2,128)} %page_mask_ref.1), custom_call_target="tpu_custom_call" | custom-call | tf_op jit(solution)/shard_map/pallas_call | solution.py:493
  2.1 0.0 copy-start
  2.1 14.5 %all_to_all.10.sent_ref.refs_0_ = bf16[32,5,2,128]{3,2,1,0:T(2,128)(2,1)S(1)} all-to-all(bf16[32,5,2,128]{3,2,1,0:T(2,128)(2,1)S(1)} %shard_map.76), channel_id=1, replica_groups=mesh['blk'=4,'group'=8] {'blk','group'}, dimensions={0} | all-to-all | bytes 163840 | tf_op jit(solution)/shard_map/all_to_all | solution.py:477
  16.7 0.1 collective-permute-start
  16.8 0.0 copy-done
  16.8 0.4 %collective-permute-start.1 = (bf16[2,128,128]{2,1,0:T(8,128)(2,1)S(1)}, bf16[2,128,128]{2,1,0:T(8,128)(2,1)S(1)}, u32[]{:S(2)}, u32[]{:S(2)}) collective-permute-start(bf16[2,128,128]{2,1,0:T(8,128)(2,1)S(1)} %copy-done), channel_id=1, source_target_pairs={{0,8},{8,0},{16,24},{24,16},{1,9},{9,1},{17,25},{25,17},{2,10},{10... | collective-permute-start | bytes 196616 | tf_op jit(solution)/shard_map/ppermute | solution.py:509
  17.2 0.5 %shard_map.77 = (bf16[256,128]{1,0:T(8,128)(2,1)S(1)}, f32[2,128,256]{2,1,0:T(8,128)S(1)}, f32[2,256]{1,0:T(2,128)S(1)}, f32[2,256]{1,0:T(2,128)S(1)}, f32[8,256...) custom-call(bf16[32,5,2,128]{3,2,1,0:T(2,128)(2,1)S(1)} %all_to_all.10.sent_ref.refs_0_, ...), custom_call_target="tpu_custom_call" | custom-call | flops 16777216 | bytes 1048576 | tf_op jit(solution)/shard_map/pallas_call | solution.py:516
  17.7 0.4 %collective-permute-done.1.refs_3_ = bf16[2,128,128]{2,1,0:T(8,128)(2,1)S(1)} collective-permute-done((bf16[2,128,128]{2,1,0:T(8,128)(2,1)S(1)}, bf16[2,128,128]{2,1,0:T(8,128)(2,1)S(1)}, u32[]{:S(2)}, u32[]{:S(2)}) %collective-permute-start.1) | collective-permute-done | bytes 65568 | tf_op jit(solution)/shard_map/ppermute | solution.py:509
  18.1 0.0 collective-permute-done.refs_1_
  18.1 0.9 %shard_map.78 = (f32[32,9,2,128]{3,2,1,0:T(2,128)S(1)}, f32[2,128,256]{2,1,0:T(8,128)S(1)}, f32[4,256]{1,0:T(4,128)S(1)}, f32[2,256]{1,0:T(2,128)S(1)}, bf16[256,128]{1,0:T(8,128)(2,1)S(1)}) custom-call(bf16[32,5,2,128]{3,2,1,0:T(2,128)(2,1)S(1)} %all_to_all.10.sent_ref.refs_0_, bf16[32,5,2,128]{3,2,1,0:T(2,128)(2,1)S(1)} %collective-permute-done.refs_1_, ...), custom_call_target="tpu_custom_call" | custom-call | tf_op jit(solution)/shard_map/pallas_call | solution.py:524
  19.0 0.1 convert_element_type.6
  19.1 9.6 %all_to_all.11 = f16[32,9,2,128]{3,2,1,0:T(2,128)(2,1)S(1)} all-to-all(f16[32,9,2,128]{3,2,1,0:T(2,128)(2,1)S(1)} %convert_element_type.6), channel_id=1, replica_groups=mesh['blk'=4,'group'=8] {'blk','group'}, dimensions={0} | all-to-all | bytes 294912 | tf_op jit(solution)/shard_map/all_to_all | solution.py:477
  28.7 0.1 convert_element_type.7.got_ref
  28.8 1.0 %shard_map.79 = (f32[1,16,128]{2,1,0:T(8,128)}, f32[2,128,128]{2,1,0:T(8,128)}, f32[1,1]{1,0:T(1,128)}) custom-call(f32[32,9,2,128]{3,2,1,0:T(2,128)S(1)} %convert_element_type.7.got_ref, f32[4,256]{1,0:T(4,128)S(1)} %get-tuple-element.29.score_ref, bf16[256,128]{1,0:T(8,128)(2,1)S(1)} %get-tuple-element.22.refs_4_.rest_0_, ...), custom_call_target="tpu_custom_call" | custom-call | tf_op jit(solution)/shard_map/pallas_call | solution.py:538
Async XLA Ops:
  2.1 14.7 %copy-start = (bf16[2,128,128]{2,1,0:T(8,128)(2,1)S(1)}, bf16[2,128,128]{2,1,0:T(8,128)(2,1)}, u32[]{:S(2)}) copy-start(bf16[2,128,128]{2,1,0:T(8,128)(2,1)} %refs_2_) | copy-start | bytes 196612
  16.7 1.4 %collective-permute-start = (bf16[32,5,2,128]{3,2,1,0:T(2,128)(2,1)S(1)}, bf16[32,5,2,128]{3,2,1,0:T(2,128)(2,1)S(1)}, u32[]{:S(2)}, u32[]{:S(2)}) collective-permute-start(bf16[32,5,2,128]{3,2,1,0:T(2,128)(2,1)S(1)} %all_to_all.10.sent_ref.refs_0_), channel_id=1, source_target_pairs={{0,8},{8,0},{16,24},{24,16},{1,9},{9,1},{17,25},{25,17},{2,10},{10... | collective-permute-start | bytes 245768 | tf_op jit(solution)/shard_map/ppermute | solution.py:508
  16.8 1.3 %collective-permute-start.1 = (bf16[2,128,128]{2,1,0:T(8,128)(2,1)S(1)}, bf16[2,128,128]{2,1,0:T(8,128)(2,1)S(1)}, u32[]{:S(2)}, u32[]{:S(2)}) collective-permute-start(bf16[2,128,128]{2,1,0:T(8,128)(2,1)S(1)} %copy-done), channel_id=1, source_target_pairs={{0,8},{8,0},{16,24},{24,16},{1,9},{9,1},{17,25},{25,17},{2,10},{10... | collective-permute-start | bytes 196616 | tf_op jit(solution)/shard_map/ppermute | solution.py:509

commit v7 on v6

--- a/solution.py
+++ b/solution.py
@@ -226,39 +226,29 @@
     return high, value - high
 
 
-def first_kernel(target_ref, queries_ref, query_mask_ref, page_mask_ref, out_ref, *scratch):
-    queries, query_mask, page_mask, sems = scratch
-    devices = out_ref.shape[0]
-    half = queries_ref.shape[1] // 2
-    members = lax.axis_size("group")
-    loads = [
-        pltpu.make_async_copy(src, dst, sems.at[i])
-        for i, (src, dst) in enumerate(
-            (
-                (queries_ref, queries),
-                (query_mask_ref, query_mask),
-                (page_mask_ref, page_mask),
-            )
-        )
-    ]
-    for load in loads:
-        load.start()
-    for load in loads:
-        load.wait()
-    alive = jnp.sum(query_mask[...].astype(jnp.float32), axis=1, keepdims=True)
+def facts_kernel(target_ref, query_mask_ref, page_mask_ref, facts_ref):
+    half = query_mask_ref.shape[1] // 2
+    alive = jnp.sum(query_mask_ref[...].astype(jnp.float32), axis=1, keepdims=True)
     kind = lax.broadcasted_iota(jnp.int32, (EXTRA, LANES), 1) % half
     number = target_ref[...].reshape(1, 1)
     facts = jnp.where(kind == 0, alive, 0.0)
     facts = jnp.where(kind == 1, (number >> 8).astype(jnp.float32), facts)
     facts = jnp.where(kind == 2, (number & 255).astype(jnp.float32), facts)
-    for page in range(page_mask.shape[0]):
-        count = jnp.sum(page_mask[page : page + 1, :].astype(jnp.float32), axis=1, keepdims=True)
+    for page in range(page_mask_ref.shape[0]):
+        count = jnp.sum(page_mask_ref[page : page + 1, :].astype(jnp.float32), axis=1, keepdims=True)
         facts = jnp.where(kind == 3 + page, count, facts)
+    facts_ref[...] = facts
+
+
+def message_kernel(facts_ref, queries_ref, out_ref):
+    devices = out_ref.shape[0]
+    half = queries_ref.shape[1] // 2
+    members = lax.axis_size("group")
     out_rows = out_ref.reshape(devices, half + EXTRA, LANES)
     for device in range(devices):
         begin = (device // members) % 2 * half
-        out_rows[device, 0:half, :] = queries[0, begin : begin + half, :]
-    out_ref[:, half // 2] = jnp.broadcast_to(facts.astype(jnp.bfloat16)[None], (devices, EXTRA, LANES))
+        out_rows[device, 0:half, :] = queries_ref[0, begin : begin + half, :]
+    out_ref[:, half // 2] = jnp.broadcast_to(facts_ref[...].astype(jnp.bfloat16)[None], (devices, EXTRA, LANES))
 
 
 def measure_pages(rows_q, vectors, flips, counts, alive, powers_ref=None):
@@ -266,10 +256,10 @@
     patch = lax.broadcasted_iota(jnp.int32, (LANES, width), 0).astype(jnp.float32)
     steep = 1.0 / (relaxation_scale_factor * math.log(2.0))
     softened, inverses, mixes = [], [], []
-    for page, (block, flipped, count) in enumerate(zip(vectors, flips, counts)):
-        similarity = lax.dot_general(
-            block, rows_q, (((1,), (1,)), ((), ())), preferred_element_type=jnp.float32
-        )
+    stack = jnp.concatenate(vectors, axis=0)
+    similarities = lax.dot_general(stack, rows_q, (((1,), (1,)), ((), ())), preferred_element_type=jnp.float32)
+    for page, (flipped, count) in enumerate(zip(flips, counts)):
+        similarity = similarities[page * LANES : (page + 1) * LANES]
         masked = jnp.where(patch < count, similarity, guarded_floor_entry)
         highest = jnp.max(masked, axis=0, keepdims=True)
         powers = jnp.exp2((masked - highest) * steep)
@@ -490,19 +480,21 @@
     vmem = pl.BlockSpec(memory_space=pltpu.VMEM)
     anywhere = pl.BlockSpec(memory_space=pl.ANY)
     params = pltpu.CompilerParams(vmem_limit_bytes=KERNEL_VMEM)
-    message = pl.pallas_call(
-        first_kernel,
-        out_shape=jax.ShapeDtypeStruct((devices, (half + EXTRA) // 2, 2, LANES), jnp.bfloat16),
-        in_specs=[vmem] + [pl.BlockSpec(memory_space=pltpu.HBM)] * 3,
+    told = pl.pallas_call(
+        facts_kernel,
+        out_shape=jax.ShapeDtypeStruct((EXTRA, LANES), jnp.float32),
+        in_specs=[vmem] * 3,
         out_specs=vmem,
         compiler_params=params,
-        scratch_shapes=[
-            pltpu.VMEM(queries.shape, jnp.bfloat16),
-            pltpu.VMEM(query_mask.shape, jnp.int32),
-            pltpu.VMEM(page_mask.shape, jnp.int32),
-            pltpu.SemaphoreType.DMA((3,)),
-        ],
-    )(positive, *[pltpu.with_memory_space_constraint(a, pltpu.HBM) for a in (queries, query_mask, page_mask)])
+        cost_estimate=pl.CostEstimate(flops=1000000, bytes_accessed=10000, transcendentals=0),
+    )(positive, query_mask, page_mask)
+    message = pl.pallas_call(
+        message_kernel,
+        out_shape=jax.ShapeDtypeStruct((devices, (half + EXTRA) // 2, 2, LANES), jnp.bfloat16),
+        in_specs=[vmem] * 2,
+        out_specs=vmem,
+        compiler_params=params,
+    )(told, queries)
     sent = exchange(message)
     sent, page_vectors = lax.optimization_barrier((sent, page_vectors))
     swapped = lax.ppermute(sent, "blk", swap)

time: 30.1 us -> 29.4 us (0.977)
  Pallas kernels: 3.21 us -> 2.51 us
    pallas_call x1 -> x2, Pallas kernels: 0.85 us -> 0.15 us  [the longest x1 0.08 us: two_exchanges(): pl.pallas_call(facts_kernel, out_shape=jax.ShapeDtypeStruct((EXTRA, LANES...]
where the time goes in v7:
time: 29.4 us; the launch traced here: 29.2 us
  blocking collectives  24.1 us (82%)
  Pallas kernels  2.51 us (9%)
  between operations  1.38 us (5%)
  starting transfers between devices  0.51 us (2%)
  waiting for transfers between devices  0.45 us (2%)
    all_to_all x2, blocking collectives, exchange(): return lax.all_to_all(blocks_to_all, ('blk', 'group'), 0, 0, tiled=True)  24.1 us
    pallas_call x1, Pallas kernels, two_exchanges(): pl.pallas_call(functools.partial(last_kernel, tokens), out_shape=(jax.Sha...  1.02 us
    pallas_call x1, Pallas kernels, two_exchanges(): pl.pallas_call(far_kernel, out_shape=(jax.ShapeDtypeStruct((devices, pair...  0.89 us
  transfers between devices with their start and end apart: 2, of which 1 were waited for; matrix products, arithmetic and copies ran while one was open for 0% of the time, Pallas kernels for 2%

profile of v7, /device:TPU:0, one launch (start us, length us, event | category | flops | bytes accessed | tf_op | source)
XLA Modules:
  0.0 29.2 jit_solution(12861912000495594988)
XLA Ops:
  0.6 0.0 copy-start.2
  0.6 0.0 copy-start.3
  0.7 0.0 copy-start.1
  1.3 0.0 copy-done.2
  1.3 0.0 copy-done.3
  1.4 0.1 shard_map.76.facts_ref
  1.4 0.0 copy-done.1
  1.4 0.1 shard_map.77
  1.5 0.0 copy-start
  1.5 14.5 %all_to_all.10.sent_ref.refs_0_ = bf16[32,5,2,128]{3,2,1,0:T(2,128)(2,1)S(1)} all-to-all(bf16[32,5,2,128]{3,2,1,0:T(2,128)(2,1)S(1)} %shard_map.77), channel_id=1, replica_groups=mesh['blk'=4,'group'=8] {'blk','group'}, dimensions={0} | all-to-all | bytes 163840 | tf_op jit(solution)/shard_map/all_to_all | solution.py:467
  16.1 0.1 collective-permute-start
  16.2 0.0 copy-done
  16.2 0.4 %collective-permute-start.1 = (bf16[2,128,128]{2,1,0:T(8,128)(2,1)S(1)}, bf16[2,128,128]{2,1,0:T(8,128)(2,1)S(1)}, u32[]{:S(2)}, u32[]{:S(2)}) collective-permute-start(bf16[2,128,128]{2,1,0:T(8,128)(2,1)S(1)} %copy-done), channel_id=1, source_target_pairs={{0,8},{8,0},{16,24},{24,16},{1,9},{9,1},{17,25},{25,17},{2,10},{10... | collective-permute-start | bytes 196616 | tf_op jit(solution)/shard_map/ppermute | solution.py:501
  16.6 0.5 %shard_map.78 = (bf16[256,128]{1,0:T(8,128)(2,1)S(1)}, f32[2,128,256]{2,1,0:T(8,128)S(1)}, f32[2,256]{1,0:T(2,128)S(1)}, f32[2,256]{1,0:T(2,128)S(1)}, f32[8,256...) custom-call(bf16[32,5,2,128]{3,2,1,0:T(2,128)(2,1)S(1)} %all_to_all.10.sent_ref.refs_0_, ...), custom_call_target="tpu_custom_call" | custom-call | flops 16777216 | bytes 1048576 | tf_op jit(solution)/shard_map/pallas_call | solution.py:508
  17.0 0.4 %collective-permute-done.1.refs_3_ = bf16[2,128,128]{2,1,0:T(8,128)(2,1)S(1)} collective-permute-done((bf16[2,128,128]{2,1,0:T(8,128)(2,1)S(1)}, bf16[2,128,128]{2,1,0:T(8,128)(2,1)S(1)}, u32[]{:S(2)}, u32[]{:S(2)}) %collective-permute-start.1) | collective-permute-done | bytes 65568 | tf_op jit(solution)/shard_map/ppermute | solution.py:501
  17.5 0.0 collective-permute-done.refs_1_
  17.5 0.9 %shard_map.79 = (f32[32,9,2,128]{3,2,1,0:T(2,128)S(1)}, f32[2,128,256]{2,1,0:T(8,128)S(1)}, f32[4,256]{1,0:T(4,128)S(1)}, f32[2,256]{1,0:T(2,128)S(1)}, bf16[256,128]{1,0:T(8,128)(2,1)S(1)}) custom-call(bf16[32,5,2,128]{3,2,1,0:T(2,128)(2,1)S(1)} %all_to_all.10.sent_ref.refs_0_, bf16[32,5,2,128]{3,2,1,0:T(2,128)(2,1)S(1)} %collective-permute-done.refs_1_, ...), custom_call_target="tpu_custom_call" | custom-call | tf_op jit(solution)/shard_map/pallas_call | solution.py:516
  18.4 0.1 convert_element_type.6
  18.5 9.6 %all_to_all.11 = f16[32,9,2,128]{3,2,1,0:T(2,128)(2,1)S(1)} all-to-all(f16[32,9,2,128]{3,2,1,0:T(2,128)(2,1)S(1)} %convert_element_type.6), channel_id=1, replica_groups=mesh['blk'=4,'group'=8] {'blk','group'}, dimensions={0} | all-to-all | bytes 294912 | tf_op jit(solution)/shard_map/all_to_all | solution.py:467
  28.1 0.1 convert_element_type.7.got_ref
  28.2 1.0 %shard_map.80 = (f32[1,16,128]{2,1,0:T(8,128)}, f32[2,128,128]{2,1,0:T(8,128)}, f32[1,1]{1,0:T(1,128)}) custom-call(f32[32,9,2,128]{3,2,1,0:T(2,128)S(1)} %convert_element_type.7.got_ref, f32[4,256]{1,0:T(4,128)S(1)} %get-tuple-element.29.score_ref, bf16[256,128]{1,0:T(8,128)(2,1)S(1)} %get-tuple-element.22.refs_4_.rest_0_, ...), custom_call_target="tpu_custom_call" | custom-call | tf_op jit(solution)/shard_map/pallas_call | solution.py:530
Async XLA Ops:
  0.6 0.7 %copy-start.2 = (s32[2,128]{1,0:T(2,128)S(1)}, s32[2,128]{1,0:T(2,128)}, u32[]{:S(2)}) copy-start(s32[2,128]{1,0:T(2,128)} %page_mask_ref.1) | copy-start | bytes 3076
  0.6 0.7 %copy-start.3 = (s32[1,16]{1,0:T(1,128)S(1)}, s32[1,16]{1,0:T(1,128)}, u32[]{:S(2)}) copy-start(s32[1,16]{1,0:T(1,128)} %query_mask_ref.1) | copy-start | bytes 196
  0.7 0.8 %copy-start.1 = (bf16[1,16,128]{2,1,0:T(8,128)(2,1)S(1)}, bf16[1,16,128]{2,1,0:T(8,128)(2,1)}, u32[]{:S(2)}) copy-start(bf16[1,16,128]{2,1,0:T(8,128)(2,1)} %queries_ref.1) | copy-start | bytes 12292
  1.5 14.7 %copy-start = (bf16[2,128,128]{2,1,0:T(8,128)(2,1)S(1)}, bf16[2,128,128]{2,1,0:T(8,128)(2,1)}, u32[]{:S(2)}) copy-start(bf16[2,128,128]{2,1,0:T(8,128)(2,1)} %refs_2_) | copy-start | bytes 196612
  16.1 1.4 %collective-permute-start = (bf16[32,5,2,128]{3,2,1,0:T(2,128)(2,1)S(1)}, bf16[32,5,2,128]{3,2,1,0:T(2,128)(2,1)S(1)}, u32[]{:S(2)}, u32[]{:S(2)}) collective-permute-start(bf16[32,5,2,128]{3,2,1,0:T(2,128)(2,1)S(1)} %all_to_all.10.sent_ref.refs_0_), channel_id=1, source_target_pairs={{0,8},{8,0},{16,24},{24,16},{1,9},{9,1},{17,25},{25,17},{2,10},{10... | collective-permute-start | bytes 245768 | tf_op jit(solution)/shard_map/ppermute | solution.py:500
  16.2 1.3 %collective-permute-start.1 = (bf16[2,128,128]{2,1,0:T(8,128)(2,1)S(1)}, bf16[2,128,128]{2,1,0:T(8,128)(2,1)S(1)}, u32[]{:S(2)}, u32[]{:S(2)}) collective-permute-start(bf16[2,128,128]{2,1,0:T(8,128)(2,1)S(1)} %copy-done), channel_id=1, source_target_pairs={{0,8},{8,0},{16,24},{24,16},{1,9},{9,1},{17,25},{25,17},{2,10},{10... | collective-permute-start | bytes 196616 | tf_op jit(solution)/shard_map/ppermute | solution.py:501
